TPU v7x, 512 devices: a whole 4x4x16 slice. The times are simulated.
512 devices in a mesh: dom: 128 (over z, y, x_lo), serve: 4 (over x_hi, core).
Axes of the slice: x: 4 (x_hi: 2, x_lo: 2; x = x_hi * 2 + x_lo), y: 4, z: 16, core: 2. Of those that a mesh axis runs over, the one named last changes fastest.
Arguments:
- source_rows: float32 [128, 4, 256, 400], P('dom', 'serve'), may hold values from -1.5 to 1.5
- source_state: float32 [128, 4, 256], P('dom', 'serve'), may hold values from 0.01 to 1
- target_rows: float32 [128, 4, 256, 400], P('dom', 'serve'), may hold values from -1.5 to 1.5
- target_state: float32 [128, 4, 256], P('dom', 'serve'), may hold values from 0.01 to 1
- relation_table: float32 [16, 400], replicated, may hold values from -4 to 4
- source_ids: int32 [128, 4, 2, 8, 128], P('dom', 'serve'), may hold values from 0 to 255
- target_ids: int32 [128, 4, 2, 8, 128], P('dom', 'serve'), may hold values from 0 to 255
- relation_ids: int32 [128, 4, 2, 8, 128], P('dom', 'serve'), may hold values from 0 to 15
- negative_block: int32 [128, 4, 2, 8], P('dom', 'serve'), may hold values from 0 to 1
- edge_counts: int32 [128, 4, 2, 8], P('dom', 'serve'), may hold values from 1 to 128, 768 in all within a row
- serving_shard: int32 [128, 4, 256], P('dom', 'serve'), may hold values from 0 to 3
- changed_rows: int32 [128, 4, 256], P('dom', 'serve'), may hold values from 0 to 1, as said below
Outputs:
- new_source: float32 [128, 4, 256, 400], P('dom', 'serve')
- new_source_state: float32 [128, 4, 256], P('dom', 'serve')
- new_target: float32 [128, 4, 256, 400], P('dom', 'serve')
- new_target_state: float32 [128, 4, 256], P('dom', 'serve')
- served: bfloat16 [128, 4, 4, 256, 400], P('dom', 'serve')
Inputs may be any that keep to these rules, and one draw needn't show every extreme that they name: `edge_counts`: for one device and step, the 8 counts sum to 768 and the largest is exactly 128. `changed_rows`: on every device at most 64 changed rows have one serving shard, and exactly 64 have some shard, the same shard for all devices of one index of dom.
All inputs are finite; a program needn't handle non-finite values.
Results may differ from a plain program's by a relative error of at most 0.001.
Values may be sent and summed in bfloat16 or wider, within the bound.
No kernel may reach another device: no remote copies, remote signals or barrier semaphores. Data moves between devices by JAX's collectives and lax.ppermute only.
A program may use at most 64 MiB of HBM per device.

v0:
```python
import jax
import jax.numpy as jnp
from jax import lax
from jax.experimental import pallas as pl
from jax.experimental.pallas import tpu as pltpu
from jax.sharding import PartitionSpec as P

LEARN_RATE = 0.1
EPSILON = 1e-08
SLOTS = 64

F32 = jnp.float32
BF16 = jnp.bfloat16
NN = ((1,), (0,))
NT = ((1,), (1,))
TN = ((0,), (0,))
LANES = 128
CHUNK = 2


def dot(a, b, dims):
    return lax.dot_general(a, b, (dims, ((), ())), preferred_element_type=F32)


def halves(x):
    high = x.astype(BF16)
    return high, (x - high.astype(F32)).astype(BF16)


def sigmoid(x):
    return 0.5 + 0.5 * jnp.tanh(0.5 * x)


def one_hot(ids, rows):
    place = lax.broadcasted_iota(jnp.int32, (rows, ids.shape[1]), 0)
    return (place == ids).astype(F32).astype(BF16)


def row_of(ids_ref, step, first):
    return jnp.concatenate([ids_ref[step, b : b + 1, :] for b in range(first, first + CHUNK)], axis=1)


def make_queries(step, source, relation3, src_ref, rel_ref, q_high, q_low, rel_out):
    high, low = halves(source)
    stacked = jnp.concatenate([high, low], axis=0)
    width = source.shape[0]
    nrel = relation3.shape[0] // 3
    for first in range(0, src_ref.shape[1], CHUNK):
        at = pl.ds(first * LANES, CHUNK * LANES)
        both = dot(stacked, one_hot(row_of(src_ref, step, first), source.shape[1]), NN)
        pick = one_hot(row_of(rel_ref, step, first), nrel)
        relation = dot(relation3, jnp.concatenate([pick, pick, pick], axis=0), TN)
        query = (both[:width] + both[width:]) * relation
        qh, ql = halves(query)
        q_high[:, at] = qh
        q_low[:, at] = ql
        rel_out[:, at] = relation


def relation_parts(relation):
    high = relation.astype(BF16)
    rest = relation - high.astype(F32)
    middle = rest.astype(BF16)
    low = (rest - middle.astype(F32)).astype(BF16)
    return jnp.concatenate([high, middle, low], axis=0)


def score_gradients(step, first, target_parts, q_high, q_low, tgt_ref, nb_ref, count_ref):
    rows = target_parts.shape[1] // 2
    at = pl.ds(first * LANES, CHUNK * LANES)
    qh = q_high[:, at]
    ql = q_low[:, at]
    both = dot(target_parts, qh, TN)
    scores = both[:rows] + both[rows:] + dot(target_parts[:, :rows], ql, TN)
    pieces = []
    lane = lax.broadcasted_iota(jnp.int32, (1, LANES), 1)
    place = lax.broadcasted_iota(jnp.int32, (rows, LANES), 0)
    for b in range(CHUNK):
        sc = scores[:, b * LANES : (b + 1) * LANES]
        hit = place == tgt_ref[step, first + b : first + b + 1, :]
        valid = (lane < count_ref[step, first + b]).astype(F32)
        positive = jnp.sum(jnp.where(hit, sc, 0.0), axis=0, keepdims=True)
        dpos = -sigmoid(-positive) * valid
        upper = nb_ref[step, first + b] == 0
        negative = jnp.where(upper, sc[:LANES], sc[LANES:])
        dneg = sigmoid(negative) * (valid * (1.0 / LANES))
        spread = jnp.concatenate([jnp.where(upper, dneg, 0.0), jnp.where(upper, 0.0, dneg)], axis=0)
        pieces.append(spread + jnp.where(hit, dpos, 0.0))
    return halves(jnp.concatenate(pieces, axis=1))


def adagrad(weights, state, gradient):
    new_state = state + jnp.sum(gradient * gradient, axis=0, keepdims=True) * (1.0 / gradient.shape[0])
    scale = LEARN_RATE / (jnp.sqrt(new_state) + EPSILON)
    return weights - gradient * scale, new_state


def target_gradient(qh, ql, gh, gl):
    width = qh.shape[0]
    both = dot(jnp.concatenate([qh, ql], axis=0), gh, NT)
    return both[:width] + both[width:] + dot(qh, gl, NT)


def source_gradient(step, first, target_stack, gh, gl, rel, src_ref):
    width = rel.shape[0]
    both = dot(target_stack, gh, NN)
    flow = (both[:width] + both[width:] + dot(target_stack[:width], gl, NN)) * rel
    fh, fl = halves(flow)
    rows = one_hot(row_of(src_ref, step, first), gh.shape[0])
    both = dot(jnp.concatenate([fh, fl], axis=0), rows, NT)
    return both[:width] + both[width:]


def prepare_kernel(source, relation, src_ref, rel_ref, q_high, q_low, rel_out):
    make_queries(0, source[...], relation_parts(relation[...]), src_ref, rel_ref, q_high, q_low, rel_out)


def target_kernel(target, state, q_high, q_low, tgt_ref, nb_ref, count_ref, new_target, new_state, g_high, g_low):
    high, low = halves(target[...])
    parts = jnp.concatenate([high, low], axis=1)
    gradient = jnp.zeros(target.shape, F32)
    for first in range(0, tgt_ref.shape[1], CHUNK):
        at = pl.ds(first * LANES, CHUNK * LANES)
        gh, gl = score_gradients(0, first, parts, q_high, q_low, tgt_ref, nb_ref, count_ref)
        g_high[:, at] = gh
        g_low[:, at] = gl
        gradient += target_gradient(q_high[:, at], q_low[:, at], gh, gl)
    new_target[...], new_state[...] = adagrad(target[...], state[...], gradient)


def source_kernel(target, source, state, relation, g_high, g_low, rel_in, src_ref, rel_ref,
                  new_source, new_state, q_high, q_low, rel_out):
    high, low = halves(target[...])
    stack = jnp.concatenate([high, low], axis=0)
    gradient = jnp.zeros(source.shape, F32)
    for first in range(0, src_ref.shape[1], CHUNK):
        at = pl.ds(first * LANES, CHUNK * LANES)
        gradient += source_gradient(0, first, stack, g_high[:, at], g_low[:, at], rel_in[:, at], src_ref)
    updated, sums = adagrad(source[...], state[...], gradient)
    new_source[...] = updated
    new_state[...] = sums
    make_queries(1, updated, relation_parts(relation[...]), src_ref, rel_ref, q_high, q_low, rel_out)


def publish(updated, shard, changed, outgoing):
    width, rows = updated.shape
    half = width // 2
    is_row = lax.broadcasted_iota(jnp.int32, (8, rows), 0)
    mine = jnp.logical_and(is_row == shard, changed == 1).astype(F32)
    before = (lax.broadcasted_iota(jnp.int32, (rows, rows), 0) < lax.broadcasted_iota(jnp.int32, (rows, rows), 1))
    rank = dot(mine.astype(BF16), before.astype(F32).astype(BF16), NN)
    slot = jnp.sum(mine * rank, axis=0, keepdims=True).astype(jnp.int32)
    code = jnp.where(changed == 1, shard * (2 * SLOTS) + slot, -1)
    shards = outgoing.shape[0]
    place = lax.broadcasted_iota(jnp.int32, (shards * 2 * SLOTS, rows), 0)
    top = (place == code).astype(F32).astype(BF16)
    bottom = jnp.logical_and(place == code + SLOTS, code >= 0).astype(F32).astype(BF16)
    number = (lax.broadcasted_iota(jnp.int32, (8, rows), 1) + 1).astype(F32)
    packed = dot(jnp.concatenate([updated[:half], number], axis=0).astype(BF16), top, NT)
    packed += dot(jnp.concatenate([updated[half:], number], axis=0).astype(BF16), bottom, NT)
    for s in range(shards):
        outgoing[s] = packed[:, s * 2 * SLOTS : (s + 1) * 2 * SLOTS].astype(BF16)


def last_source_kernel(target, source, state, q_high, q_low, rel_in, src_ref, tgt_ref, nb_ref, count_ref, shard, changed,
                       new_source, new_state, g_high, g_low, outgoing):
    high, low = halves(target[...])
    parts = jnp.concatenate([high, low], axis=1)
    stack = jnp.concatenate([high, low], axis=0)
    gradient = jnp.zeros(source.shape, F32)
    for first in range(0, src_ref.shape[1], CHUNK):
        at = pl.ds(first * LANES, CHUNK * LANES)
        gh, gl = score_gradients(1, first, parts, q_high, q_low, tgt_ref, nb_ref, count_ref)
        g_high[:, at] = gh
        g_low[:, at] = gl
        gradient += source_gradient(1, first, stack, gh, gl, rel_in[:, at], src_ref)
    updated, sums = adagrad(source[...], state[...], gradient)
    new_source[...] = updated
    new_state[...] = sums
    publish(updated, shard[...], changed[...], outgoing)


def last_target_kernel(target, state, q_high, q_low, g_high, g_low, new_target, new_state):
    gradient = jnp.zeros(target.shape, F32)
    step = CHUNK * LANES
    for first in range(0, q_high.shape[1], step):
        at = pl.ds(first, step)
        gradient += target_gradient(q_high[:, at], q_low[:, at], g_high[:, at], g_low[:, at])
    new_target[...], new_state[...] = adagrad(target[...], state[...], gradient)


def serve_kernel(incoming, served):
    shards, packed_rows, lanes = incoming.shape
    half = served.shape[1] // 2
    rows = served.shape[2]
    lane = lax.broadcasted_iota(jnp.int32, (rows, lanes), 1)
    number = (lax.broadcasted_iota(jnp.int32, (rows, lanes), 0) + 1).astype(F32)
    for s in range(shards):
        block = incoming[s]
        index = block[half : half + 8].astype(F32)[:1]
        match = number == index
        top = jnp.logical_and(match, lane < SLOTS).astype(F32)
        bottom = jnp.logical_and(match, lane >= SLOTS).astype(F32)
        spread = dot(block, jnp.concatenate([top, bottom], axis=0).astype(BF16), NT)
        served[s] = jnp.concatenate([spread[:half, :rows], spread[:half, rows:]], axis=0).astype(BF16)


VMEM = pl.BlockSpec(memory_space=pltpu.VMEM)
SMEM = pl.BlockSpec(memory_space=pltpu.SMEM)


def call(kernel, outs, args, scalars=(), flops=10**9):
    return pl.pallas_call(
        kernel,
        out_shape=[jax.ShapeDtypeStruct(shape, kind) for shape, kind in outs],
        in_specs=[SMEM if i in scalars else VMEM for i in range(len(args))],
        out_specs=[VMEM] * len(outs),
        compiler_params=pltpu.CompilerParams(vmem_limit_bytes=40 * 2**20),
        cost_estimate=pl.CostEstimate(flops=flops, bytes_accessed=4 * 2**20, transcendentals=2**17),
    )(*args)


def from_behind(block, axis, distance):
    devices = range(lax.axis_size(axis))
    route = [((i - distance) % len(devices), i) for i in devices]
    return lax.ppermute(block, axis, route)


def on_device(
    source_rows,
    source_state,
    target_rows,
    target_state,
    relation_table,
    source_ids,
    target_ids,
    relation_ids,
    negative_block,
    edge_counts,
    serving_shard,
    changed_rows,
):
    source = jnp.swapaxes(source_rows[0, 0], 0, 1)
    target = jnp.swapaxes(target_rows[0, 0], 0, 1)
    source_sums, target_sums = source_state[0], target_state[0]
    src, tgt, rel = source_ids[0, 0], target_ids[0, 0], relation_ids[0, 0]
    negatives, counts = negative_block[0, 0], edge_counts[0, 0]
    width, rows = source.shape
    edges = src.shape[1] * src.shape[2]
    shards = lax.axis_size("serve")
    matrix, line = ((width, rows), F32), ((1, rows), F32)
    edge16, edge32, grad16 = ((width, edges), BF16), ((width, edges), F32), ((rows, edges), BF16)

    target = from_behind(target, "dom", 1)
    target_sums = from_behind(target_sums, "dom", 1)
    q_high, q_low, relation = call(prepare_kernel, [edge16, edge16, edge32], (source, relation_table, src, rel))
    moved, moved_sums, g_high, g_low = call(
        target_kernel, [matrix, line, grad16, grad16],
        (target, target_sums, q_high, q_low, tgt, negatives, counts), (5, 6))
    moved = from_behind(moved, "dom", 1)
    moved_sums = from_behind(moved_sums, "dom", 1)
    source, source_sums, q_high, q_low, relation = call(
        source_kernel, [matrix, line, edge16, edge16, edge32],
        (target, source, source_sums, relation_table, g_high, g_low, relation, src, rel))
    target, target_sums = moved, moved_sums
    source, source_sums, g_high, g_low, outgoing = call(
        last_source_kernel, [matrix, line, grad16, grad16, ((shards, width // 2 + 8, 2 * SLOTS), BF16)],
        (target, source, source_sums, q_high, q_low, relation, src, tgt, negatives, counts, serving_shard[0], changed_rows[0]),
        (8, 9))
    incoming = lax.all_to_all(outgoing, "serve", split_axis=0, concat_axis=0, tiled=True)
    target, target_sums = call(last_target_kernel, [matrix, line], (target, target_sums, q_high, q_low, g_high, g_low))
    served = call(serve_kernel, [((shards, width, rows), BF16)], (incoming,))[0]
    return (
        jnp.swapaxes(source, 0, 1)[None, None],
        source_sums[None],
        jnp.swapaxes(target, 0, 1)[None, None],
        target_sums[None],
        jnp.swapaxes(served, 1, 2)[None, None],
    )


def solution(mesh):
    return jax.shard_map(
        on_device,
        mesh=mesh,
        in_specs=(
            P("dom", "serve", None, None),
            P("dom", "serve", None),
            P("dom", "serve", None, None),
            P("dom", "serve", None),
            P(),
            P("dom", "serve", None, None, None),
            P("dom", "serve", None, None, None),
            P("dom", "serve", None, None, None),
            P("dom", "serve", None, None),
            P("dom", "serve", None, None),
            P("dom", "serve", None),
            P("dom", "serve", None),
        ),
        out_specs=(
            P("dom", "serve", None, None),
            P("dom", "serve", None),
            P("dom", "serve", None, None),
            P("dom", "serve", None),
            P("dom", "serve", None, None, None),
        ),
        check_vma=False,
    )
```

profile of v0, /device:TPU:1, one launch (start us, length us, event | category | flops | bytes accessed | tf_op | source)
XLA Modules:
  0.0 67.2 jit_solution(13715224458173327476)
XLA Ops:
  0.6 3.9 %collective-permute-start = (f32[400,256]{1,0:T(8,128)}, f32[400,256]{1,0:T(8,128)S(1)}, u32[]{:S(2)}, u32[]{:S(2)}) collective-permute-start(f32[400,256]{1,0:T(8,128)} %bitcast.42), channel_id=1, source_target_pairs={{508,0},{0,4},{4,8},{8,12},{12,16},{16,20},{20,24},{24,28},{28,32}... | collective-permute-start | bytes 1228808 | tf_op jit(solution)/shard_map/ppermute | solution.py:226
  4.6 3.2 %collective-permute-start.1 = (f32[1,256]{1,0:T(1,128)}, f32[1,256]{1,0:T(1,128)S(1)}, u32[]{:S(2)}, u32[]{:S(2)}) collective-permute-start(f32[1,256]{1,0:T(1,128)} %bitcast.44), channel_id=1, source_target_pairs={{508,0},{0,4},{4,8},{8,12},{12,16},{16,20},{20,24},{24,28},{28,32}... | collective-permute-start | bytes 3080 | tf_op jit(solution)/shard_map/ppermute | solution.py:226
  7.8 0.0 copy-start
  7.8 0.7 %copy-done = s32[1,1,2,8,128]{4,3,2,1,0:T(8,128)S(1)} copy-done((s32[1,1,2,8,128]{4,3,2,1,0:T(8,128)S(1)}, s32[1,1,2,8,128]{4,3,2,1,0:T(8,128)}, u32[]{:S(2)}) %copy-start) | copy-done | bytes 8216
  8.5 0.0 copy-start.7
  8.5 1.0 %copy-done.7 = f32[1,1,256,400]{2,3,1,0:T(8,128)S(1)} copy-done((f32[1,1,256,400]{2,3,1,0:T(8,128)S(1)}, f32[1,1,256,400]{2,3,1,0:T(8,128)}, u32[]{:S(2)}) %copy-start.7) | copy-done | bytes 409624
  9.5 0.0 copy-start.9
  9.5 0.8 %copy-done.9 = f32[16,400]{1,0:T(8,128)S(1)} copy-done((f32[16,400]{1,0:T(8,128)S(1)}, f32[16,400]{1,0:T(8,128)}, u32[]{:S(2)}) %copy-start.9) | copy-done | bytes 25624
  10.2 0.0 copy-start.11
  10.2 0.7 %copy-done.11 = s32[1,1,2,8,128]{4,3,2,1,0:T(8,128)S(1)} copy-done((s32[1,1,2,8,128]{4,3,2,1,0:T(8,128)S(1)}, s32[1,1,2,8,128]{4,3,2,1,0:T(8,128)}, u32[]{:S(2)}) %copy-start.11) | copy-done | bytes 8216
  10.9 0.0 copy-start.2
  10.9 0.0 copy-start.3
  10.9 0.0 copy-start.4
  10.9 0.8 %shard_map.155 = (bf16[400,1024]{1,0:T(8,128)(2,1)S(1)}, bf16[400,1024]{1,0:T(8,128)(2,1)S(1)}, f32[400,1024]{1,0:T(8,128)S(1)}) custom-call(f32[400,256]{1,0:T(8,128)S(1)} %bitcast.37, f32[16,400]{1,0:T(8,128)S(1)} %copy-done.9, s32[2,8,128]{2,1,0:T(8,128)S(1)} %bitcast.26, s32[2,8,128]{2,1,0:T(8,128)S(1)} %bitcast.39), custom_call_target="tpu_custom_call" | custom-call | flops 1000000000 | bytes 4194304 | tf_op jit(solution)/shard_map/pallas_call | solution.py:213
  11.8 13.6 %collective-permute-done.1.state = f32[1,256]{1,0:T(1,128)S(1)} collective-permute-done((f32[1,256]{1,0:T(1,128)}, f32[1,256]{1,0:T(1,128)S(1)}, u32[]{:S(2)}, u32[]{:S(2)}) %collective-permute-start.1) | collective-permute-done | bytes 1056 | tf_op jit(solution)/shard_map/ppermute | solution.py:226
  25.4 0.0 collective-permute-done.target
  25.4 0.0 copy-done.2
  25.4 0.0 copy-done.3
  25.4 0.0 copy-done.4
  25.4 0.0 copy-start.1
  25.4 0.0 copy-start.8
  25.4 0.0 copy-start.10
  25.4 0.0 copy-start.12
  25.4 0.0 copy-start.13
  25.5 3.2 %shard_map.156 = (f32[400,256]{1,0:T(8,128)S(1)}, f32[1,256]{1,0:T(1,128)S(1)}, bf16[256,1024]{1,0:T(8,128)(2,1)S(1)}, bf16[256,1024]{1,0:T(8,128)(2,1)S(1)}) custom-call(f32[400,256]{1,0:T(8,128)S(1)} %collective-permute-done.target, f32[1,256]{1,0:T(1,128)S(1)} %collective-permute-done.1.state, bf16[400,1024]{1,0:T(8,128)(2,1)S(1)} %get-tuple-element.24.q_high, ...), custom_call_target="tpu_custom_call" | custom-call | flops 1000000000 | bytes 4194304 | tf_op jit(solution)/shard_map/pallas_call | solution.py:213
  28.7 1.9 %collective-permute-start.2 = (f32[400,256]{1,0:T(8,128)S(1)}, f32[400,256]{1,0:T(8,128)S(1)}, u32[]{:S(2)}, u32[]{:S(2)}) collective-permute-start(f32[400,256]{1,0:T(8,128)S(1)} %get-tuple-element.26), channel_id=1, source_target_pairs={{508,0},{0,4},{4,8},{8,12},{12,16},{16,20},{20,24},{24,28},{28,32}... | collective-permute-start | bytes 1228808 | tf_op jit(solution)/shard_map/ppermute | solution.py:226
  30.6 0.0 copy-done.1
  30.7 0.0 copy-done.8
  30.7 0.0 copy-done.10
  30.7 0.0 copy-done.12
  30.7 0.0 copy-done.13
  30.7 0.0 copy-start.5
  30.7 0.0 copy-start.6
  30.7 2.7 %shard_map.157 = (f32[400,256]{1,0:T(8,128)S(1)}, f32[1,256]{1,0:T(1,128)S(1)}, bf16[400,1024]{1,0:T(8,128)(2,1)S(1)}, bf16[400,1024]{1,0:T(8,128)(2,1)S(1)}, f32[400,1024]{1,0:T(8,128)S(1)}) custom-call(f32[400,256]{1,0:T(8,128)S(1)} %collective-permute-done.target, f32[400,256]{1,0:T(8,128)S(1)} %bitcast.38, f32[1,256]{1,0:T(1,128)S(1)} %bitcast.41, ...), custom_call_target="tpu_custom_call" | custom-call | flops 1000000000 | bytes 4194304 | tf_op jit(solution)/shard_map/pallas_call | solution.py:213
  33.4 11.1 %collective-permute-done.2.target = f32[400,256]{1,0:T(8,128)S(1)} collective-permute-done((f32[400,256]{1,0:T(8,128)S(1)}, f32[400,256]{1,0:T(8,128)S(1)}, u32[]{:S(2)}, u32[]{:S(2)}) %collective-permute-start.2) | collective-permute-done | bytes 409632 | tf_op jit(solution)/shard_map/ppermute | solution.py:226
  44.5 0.0 copy-done.5
  44.5 0.0 copy-done.6
  44.5 5.0 %shard_map.158 = (f32[400,256]{1,0:T(8,128)}, f32[1,256]{1,0:T(1,128)}, bf16[256,1024]{1,0:T(8,128)(2,1)S(1)}, bf16[256,1024]{1,0:T(8,128)(2,1)S(1)}, bf16[4,208,128]{2,1,0:T(8,128)(2,1)}) custom-call(f32[400,256]{1,0:T(8,128)S(1)} %collective-permute-done.2.target, f32[400,256]{1,0:T(8,128)S(1)} %get-tuple-element.30.source, ...), custom_call_target="tpu_custom_call" | custom-call | flops 1000000000 | bytes 4194304 | tf_op jit(solution)/shard_map/pallas_call | solution.py:213
  49.5 6.2 %all-to-all-start = ((bf16[4,208,128]{2,1,0:T(8,128)(2,1)}), bf16[4,208,128]{2,1,0:T(8,128)(2,1)S(1)}, u32[]{:S(2)}, u32[]{:S(2)}) async-start(bf16[4,208,128]{2,1,0:T(8,128)(2,1)} %get-tuple-element.42), calls=%async_computation | async-start | bytes 425984 | tf_op jit(solution)/shard_map/all_to_all | solution.py:270
  55.7 1.9 %collective-permute-start.3 = (f32[1,256]{1,0:T(1,128)S(1)}, f32[1,256]{1,0:T(1,128)S(1)}, u32[]{:S(2)}, u32[]{:S(2)}) collective-permute-start(f32[1,256]{1,0:T(1,128)S(1)} %get-tuple-element.37), channel_id=1, source_target_pairs={{508,0},{0,4},{4,8},{8,12},{12,16},{16,20},{20,24},{24,28},{28,32}... | collective-permute-start | bytes 3080 | tf_op jit(solution)/shard_map/ppermute | solution.py:226
  57.6 6.6 %collective-permute-done.3.state = f32[1,256]{1,0:T(1,128)S(1)} collective-permute-done((f32[1,256]{1,0:T(1,128)S(1)}, f32[1,256]{1,0:T(1,128)S(1)}, u32[]{:S(2)}, u32[]{:S(2)}) %collective-permute-start.3) | collective-permute-done | bytes 1056 | tf_op jit(solution)/shard_map/ppermute | solution.py:226
  64.2 1.7 %shard_map.159 = (f32[400,256]{1,0:T(8,128)}, f32[1,256]{1,0:T(1,128)}) custom-call(f32[400,256]{1,0:T(8,128)S(1)} %collective-permute-done.2.target, f32[1,256]{1,0:T(1,128)S(1)} %collective-permute-done.3.state, bf16[400,1024]{1,0:T(8,128)(2,1)S(1)} %get-tuple-element.32.q_high, bf16[400,1024]{1,0:T(8,128)(2,1)S(1)} %get-tuple-element.33.q_low, ...), custom_call_target="tpu_custom_call" | custom-call | flops 1000000000 | bytes 4194304 | tf_op jit(solution)/shard_map/pallas_call | solution.py:213
  65.9 0.0 all-to-all-done.incoming
  65.9 1.3 %shard_map.160 = bf16[4,400,256]{2,1,0:T(8,128)(2,1)} custom-call(bf16[4,208,128]{2,1,0:T(8,128)(2,1)S(1)} %all-to-all-done.incoming), custom_call_target="tpu_custom_call" | custom-call | flops 1000000000 | bytes 4194304 | tf_op jit(solution)/shard_map/pallas_call | solution.py:213
Async XLA Ops:
  0.6 24.7 %collective-permute-start = (f32[400,256]{1,0:T(8,128)}, f32[400,256]{1,0:T(8,128)S(1)}, u32[]{:S(2)}, u32[]{:S(2)}) collective-permute-start(f32[400,256]{1,0:T(8,128)} %bitcast.42), channel_id=1, source_target_pairs={{508,0},{0,4},{4,8},{8,12},{12,16},{16,20},{20,24},{24,28},{28,32}... | collective-permute-start | bytes 1228808 | tf_op jit(solution)/shard_map/ppermute | solution.py:226
  4.6 20.8 %collective-permute-start.1 = (f32[1,256]{1,0:T(1,128)}, f32[1,256]{1,0:T(1,128)S(1)}, u32[]{:S(2)}, u32[]{:S(2)}) collective-permute-start(f32[1,256]{1,0:T(1,128)} %bitcast.44), channel_id=1, source_target_pairs={{508,0},{0,4},{4,8},{8,12},{12,16},{16,20},{20,24},{24,28},{28,32}... | collective-permute-start | bytes 3080 | tf_op jit(solution)/shard_map/ppermute | solution.py:226
  7.8 0.7 %copy-start = (s32[1,1,2,8,128]{4,3,2,1,0:T(8,128)S(1)}, s32[1,1,2,8,128]{4,3,2,1,0:T(8,128)}, u32[]{:S(2)}) copy-start(s32[1,1,2,8,128]{4,3,2,1,0:T(8,128)} %param.17) | copy-start | bytes 24580
  8.5 1.0 %copy-start.7 = (f32[1,1,256,400]{2,3,1,0:T(8,128)S(1)}, f32[1,1,256,400]{2,3,1,0:T(8,128)}, u32[]{:S(2)}) copy-start(f32[1,1,256,400]{2,3,1,0:T(8,128)} %param.12) | copy-start | bytes 1228804
  9.5 0.8 %copy-start.9 = (f32[16,400]{1,0:T(8,128)S(1)}, f32[16,400]{1,0:T(8,128)}, u32[]{:S(2)}) copy-start(f32[16,400]{1,0:T(8,128)} %relation.3) | copy-start | bytes 76804
  10.2 0.7 %copy-start.11 = (s32[1,1,2,8,128]{4,3,2,1,0:T(8,128)S(1)}, s32[1,1,2,8,128]{4,3,2,1,0:T(8,128)}, u32[]{:S(2)}) copy-start(s32[1,1,2,8,128]{4,3,2,1,0:T(8,128)} %param.19) | copy-start | bytes 24580
  10.9 14.4 %copy-start.2 = (s32[1,1,2,8,128]{4,3,2,1,0:T(8,128)S(1)}, s32[1,1,2,8,128]{4,3,2,1,0:T(8,128)}, u32[]{:S(2)}) copy-start(s32[1,1,2,8,128]{4,3,2,1,0:T(8,128)} %param.18) | copy-start | bytes 24580
  10.9 14.4 %copy-start.3 = (s32[1,1,2,8]{3,2,1,0:T(2,128)S(1)}, s32[1,1,2,8]{3,2,1,0:T(2,128)}, u32[]{:S(2)}) copy-start(s32[1,1,2,8]{3,2,1,0:T(2,128)} %param.20) | copy-start | bytes 196
  10.9 14.5 %copy-start.4 = (s32[1,1,2,8]{3,2,1,0:T(2,128)S(1)}, s32[1,1,2,8]{3,2,1,0:T(2,128)}, u32[]{:S(2)}) copy-start(s32[1,1,2,8]{3,2,1,0:T(2,128)} %param.21) | copy-start | bytes 196
  25.4 5.2 %copy-start.1 = (s32[1,1,2,8,128]{4,3,2,1,0:T(8,128)S(1)}, s32[1,1,2,8,128]{4,3,2,1,0:T(8,128)}, u32[]{:S(2)}) copy-start(s32[1,1,2,8,128]{4,3,2,1,0:T(8,128)} %param.17) | copy-start | bytes 24580
  25.4 5.2 %copy-start.8 = (f32[1,1,256,400]{2,3,1,0:T(8,128)S(1)}, f32[1,1,256,400]{2,3,1,0:T(8,128)}, u32[]{:S(2)}) copy-start(f32[1,1,256,400]{2,3,1,0:T(8,128)} %param.12) | copy-start | bytes 1228804
  25.4 5.2 %copy-start.10 = (f32[16,400]{1,0:T(8,128)S(1)}, f32[16,400]{1,0:T(8,128)}, u32[]{:S(2)}) copy-start(f32[16,400]{1,0:T(8,128)} %relation.3) | copy-start | bytes 76804
  25.4 5.2 %copy-start.12 = (s32[1,1,2,8,128]{4,3,2,1,0:T(8,128)S(1)}, s32[1,1,2,8,128]{4,3,2,1,0:T(8,128)}, u32[]{:S(2)}) copy-start(s32[1,1,2,8,128]{4,3,2,1,0:T(8,128)} %param.19) | copy-start | bytes 24580
  25.4 5.2 %copy-start.13 = (f32[1,1,256]{2,1,0:T(1,128)S(1)}, f32[1,1,256]{2,1,0:T(1,128)}, u32[]{:S(2)}) copy-start(f32[1,1,256]{2,1,0:T(1,128)} %param.13) | copy-start | bytes 3076
  28.7 15.8 %collective-permute-start.2 = (f32[400,256]{1,0:T(8,128)S(1)}, f32[400,256]{1,0:T(8,128)S(1)}, u32[]{:S(2)}, u32[]{:S(2)}) collective-permute-start(f32[400,256]{1,0:T(8,128)S(1)} %get-tuple-element.26), channel_id=1, source_target_pairs={{508,0},{0,4},{4,8},{8,12},{12,16},{16,20},{20,24},{24,28},{28,32}... | collective-permute-start | bytes 1228808 | tf_op jit(solution)/shard_map/ppermute | solution.py:226
  30.7 13.8 %copy-start.5 = (s32[1,1,256]{2,1,0:T(1,128)S(1)}, s32[1,1,256]{2,1,0:T(1,128)}, u32[]{:S(2)}) copy-start(s32[1,1,256]{2,1,0:T(1,128)} %param.22) | copy-start | bytes 3076
  30.7 13.8 %copy-start.6 = (s32[1,1,256]{2,1,0:T(1,128)S(1)}, s32[1,1,256]{2,1,0:T(1,128)}, u32[]{:S(2)}) copy-start(s32[1,1,256]{2,1,0:T(1,128)} %param.23) | copy-start | bytes 3076
  49.5 16.4 %all-to-all-start = ((bf16[4,208,128]{2,1,0:T(8,128)(2,1)}), bf16[4,208,128]{2,1,0:T(8,128)(2,1)S(1)}, u32[]{:S(2)}, u32[]{:S(2)}) async-start(bf16[4,208,128]{2,1,0:T(8,128)(2,1)} %get-tuple-element.42), calls=%async_computation | async-start | bytes 425984 | tf_op jit(solution)/shard_map/all_to_all | solution.py:270
  55.7 8.5 %collective-permute-start.3 = (f32[1,256]{1,0:T(1,128)S(1)}, f32[1,256]{1,0:T(1,128)S(1)}, u32[]{:S(2)}, u32[]{:S(2)}) collective-permute-start(f32[1,256]{1,0:T(1,128)S(1)} %get-tuple-element.37), channel_id=1, source_target_pairs={{508,0},{0,4},{4,8},{8,12},{12,16},{16,20},{20,24},{24,28},{28,32}... | collective-permute-start | bytes 3080 | tf_op jit(solution)/shard_map/ppermute | solution.py:226
where the time goes:
time: 67.8 us; the launch traced here: 67.2 us
  waiting for transfers between devices  31.3 us (46%)
  starting transfers between devices  17.1 us (25%)
  Pallas kernels  14.7 us (22%)
  local copies, waits for them, and re-layouts  3.2 us (5%)
  between operations  0.81 us (1%)
    ppermute x4, waiting for transfers between devices, from_behind(): return lax.ppermute(block, axis, route)  31.3 us
    pallas_call x6, Pallas kernels, call(): pl.pallas_call(kernel, out_shape=[jax.ShapeDtypeStruct(shape, kind) for s...  14.7 us
    ppermute x4, starting transfers between devices, from_behind(): return lax.ppermute(block, axis, route)  11 us
    all_to_all x1, starting transfers between devices, on_device(): lax.all_to_all(outgoing, 'serve', split_axis=0, concat_axis=0, tiled=True)  6.18 us
    unnamed x28, local copies, waits for them, and re-layouts  3.2 us
  transfers between devices with their start and end apart: 5, of which 3 were waited for; matrix products, arithmetic and copies ran while one was open for 0% of the time, Pallas kernels for 8%

commit v1 on v0

v1 whole, which is shorter than its diff:
```python
import jax
import jax.numpy as jnp
from jax import lax
from jax.experimental import pallas as pl
from jax.experimental.pallas import tpu as pltpu
from jax.sharding import PartitionSpec as P

LEARN_RATE = 0.1
EPSILON = 1e-08
SLOTS = 64

F32 = jnp.float32
BF16 = jnp.bfloat16
NN = ((1,), (0,))
NT = ((1,), (1,))
TN = ((0,), (0,))
LANES = 128
CHUNK = 256
LIVE = 768
SCALE_UNIT = 16384.0
CODE_MAX = 32767.0
TAIL = 16


def dot(a, b, dims):
    return lax.dot_general(a, b, (dims, ((), ())), preferred_element_type=F32)


def halves(x):
    high = x.astype(BF16)
    return high, (x - high.astype(F32)).astype(BF16)


def sigmoid(x):
    return 0.5 + 0.5 * jnp.tanh(0.5 * x)


def one_hot(ids, rows):
    place = lax.broadcasted_iota(jnp.int32, (rows, ids.shape[1]), 0)
    return (place == ids).astype(F32).astype(BF16)


def compact(step, src_ref, tgt_ref, rel_ref, nb_ref, count_ref):
    blocks, lanes = src_ref.shape[1:]
    stack = jnp.concatenate([src_ref[step], tgt_ref[step], rel_ref[step], jnp.zeros_like(src_ref[step])], axis=0)
    stack = stack.astype(F32)
    row = lax.broadcasted_iota(jnp.int32, stack.shape, 0)
    edge = lax.broadcasted_iota(jnp.int32, (lanes, LIVE), 0)
    apart = lax.broadcasted_iota(jnp.int32, (lanes, LIVE), 1) - edge
    packed = jnp.zeros((stack.shape[0], LIVE), F32)
    start = 0
    for b in range(blocks):
        count = count_ref[step, b]
        block = nb_ref[step, b].astype(F32)
        mine = jnp.where(row % blocks == b, stack + jnp.where(row >= 3 * blocks, block, 0.0), 0.0)
        to = jnp.logical_and(apart == start, edge < count)
        packed += dot(mine.astype(BF16), to.astype(F32).astype(BF16), NN)
        start = start + count
    return [
        jnp.sum(packed[i * blocks : (i + 1) * blocks], axis=0, keepdims=True).astype(jnp.int32) for i in range(4)
    ]


def pick_rows(rows, values, shape):
    row = lax.broadcasted_iota(jnp.int32, shape, 0)
    out = jnp.zeros(shape, jnp.int32)
    for i, value in zip(rows, values):
        out = jnp.where(row == i, value, out)
    return out


def coded(x):
    largest = jnp.max(jnp.abs(x), axis=0, keepdims=True)
    unit = jnp.floor(largest * SCALE_UNIT) + 1.0
    code = jnp.floor(x * ((CODE_MAX * SCALE_UNIT) / unit) + 0.5)
    return code.astype(jnp.int32), unit.astype(jnp.int32)


def decoded(codes, unit):
    return codes.astype(F32) * (unit.astype(F32) * (1.0 / (CODE_MAX * SCALE_UNIT)))


def relation_parts(relation):
    high = relation.astype(BF16)
    rest = relation - high.astype(F32)
    middle = rest.astype(BF16)
    low = (rest - middle.astype(F32)).astype(BF16)
    return jnp.concatenate([high, middle, low], axis=0)


def queries(source_stack, relation3, src, rel):
    width = source_stack.shape[0] // 2
    relations = relation3.shape[0] // 3
    both = dot(source_stack, one_hot(src, source_stack.shape[1]), NN)
    pick = one_hot(rel, relations)
    relation = dot(relation3, jnp.concatenate([pick, pick, pick], axis=0), TN)
    qh, ql = halves((both[:width] + both[width:]) * relation)
    return qh, ql, relation


def score_gradients(target_parts, qh, ql, tgt, block):
    rows = target_parts.shape[1] // 2
    lanes = tgt.shape[1]
    both = dot(target_parts, qh, TN)
    scores = both[:rows] + both[rows:] + dot(target_parts[:, :rows], ql, TN)
    hit = lax.broadcasted_iota(jnp.int32, (rows, lanes), 0) == tgt
    positive = jnp.sum(jnp.where(hit, scores, 0.0), axis=0, keepdims=True)
    dpos = -sigmoid(-positive)
    upper = jnp.broadcast_to(block, (LANES, lanes)) == 0
    negative = jnp.where(upper, scores[:LANES], scores[LANES:])
    dneg = sigmoid(negative) * (1.0 / LANES)
    spread = jnp.concatenate([jnp.where(upper, dneg, 0.0), jnp.where(upper, 0.0, dneg)], axis=0)
    return halves(spread + jnp.where(hit, dpos, 0.0))


def adagrad(weights, state, gradient):
    new_state = state + jnp.sum(gradient * gradient, axis=0, keepdims=True) * (1.0 / gradient.shape[0])
    scale = LEARN_RATE / (jnp.sqrt(new_state) + EPSILON)
    return weights - gradient * scale, new_state


def target_gradient(qh, ql, gh, gl):
    width = qh.shape[0]
    both = dot(jnp.concatenate([qh, ql], axis=0), gh, NT)
    return both[:width] + both[width:] + dot(qh, gl, NT)


def source_gradient(target_stack, gh, gl, relation, src):
    width = relation.shape[0]
    both = dot(target_stack, gh, NN)
    flow = (both[:width] + both[width:] + dot(target_stack[:width], gl, NN)) * relation
    fh, fl = halves(flow)
    both = dot(jnp.concatenate([fh, fl], axis=0), one_hot(src, gh.shape[0]), NT)
    return both[:width] + both[width:]


def encode_target_kernel(target, state, payload):
    codes, unit = coded(target[...])
    scaled = state[...] * SCALE_UNIT
    whole = jnp.floor(scaled)
    part = jnp.floor((scaled - whole) * SCALE_UNIT + 0.5)
    tail = pick_rows(
        range(3), [unit, whole.astype(jnp.int32), part.astype(jnp.int32)], (TAIL, target.shape[1]))
    payload[...] = jnp.concatenate([codes, tail], axis=0).astype(jnp.int16)


def encode_source_kernel(source, src_ref, tgt_ref, rel_ref, nb_ref, count_ref, payload, ids_now, ids_next):
    codes, unit = coded(source[...])
    rows = source.shape[1]
    ids = compact(0, src_ref, tgt_ref, rel_ref, nb_ref, count_ref)
    ids_now[...] = pick_rows(range(4), ids, ids_now.shape)
    pieces = [i[:, at : at + rows] for i in ids for at in range(0, LIVE, rows)]
    tail = pick_rows(range(TAIL), [unit] + pieces, (TAIL, rows))
    payload[...] = jnp.concatenate([codes, tail], axis=0).astype(jnp.int16)
    ids = compact(1, src_ref, tgt_ref, rel_ref, nb_ref, count_ref)
    ids_next[...] = pick_rows(range(4), ids, ids_next.shape)


def query_kernel(source, relation, ids, q_high, q_low, rel_out):
    stack = jnp.concatenate(halves(source[...]), axis=0)
    relation3 = relation_parts(relation[...])
    for first in range(0, LIVE, CHUNK):
        at = pl.ds(first, CHUNK)
        q_high[:, at], q_low[:, at], rel_out[:, at] = queries(stack, relation3, ids[0:1, at], ids[2:3, at])


def source_kernel(payload, source, state, relation, ids, ids_next, q_high, q_low, rel_in,
                  new_source, new_state, next_high, next_low, next_rel):
    width = source.shape[0]
    packed = payload[...].astype(jnp.int32)
    high, low = halves(decoded(packed[:width], packed[width : width + 1]))
    parts = jnp.concatenate([high, low], axis=1)
    stack = jnp.concatenate([high, low], axis=0)
    gradient = jnp.zeros(source.shape, F32)
    for first in range(0, LIVE, CHUNK):
        at = pl.ds(first, CHUNK)
        gh, gl = score_gradients(parts, q_high[:, at], q_low[:, at], ids[1:2, at], ids[3:4, at])
        gradient += source_gradient(stack, gh, gl, rel_in[:, at], ids[0:1, at])
    updated, sums = adagrad(source[...], state[...], gradient)
    new_source[...] = updated
    new_state[...] = sums
    stack = jnp.concatenate(halves(updated), axis=0)
    relation3 = relation_parts(relation[...])
    for first in range(0, LIVE, CHUNK):
        at = pl.ds(first, CHUNK)
        next_high[:, at], next_low[:, at], next_rel[:, at] = queries(
            stack, relation3, ids_next[0:1, at], ids_next[2:3, at])


def publish(updated, shard, changed, outgoing):
    width, rows = updated.shape
    half = width // 2
    is_row = lax.broadcasted_iota(jnp.int32, (8, rows), 0)
    mine = jnp.logical_and(is_row == shard, changed == 1).astype(F32)
    before = (lax.broadcasted_iota(jnp.int32, (rows, rows), 0) < lax.broadcasted_iota(jnp.int32, (rows, rows), 1))
    rank = dot(mine.astype(BF16), before.astype(F32).astype(BF16), NN)
    slot = jnp.sum(mine * rank, axis=0, keepdims=True).astype(jnp.int32)
    code = jnp.where(changed == 1, shard * (2 * SLOTS) + slot, -1)
    shards = outgoing.shape[0]
    place = lax.broadcasted_iota(jnp.int32, (shards * 2 * SLOTS, rows), 0)
    top = (place == code).astype(F32).astype(BF16)
    bottom = jnp.logical_and(place == code + SLOTS, code >= 0).astype(F32).astype(BF16)
    number = (lax.broadcasted_iota(jnp.int32, (8, rows), 1) + 1).astype(F32)
    packed = dot(jnp.concatenate([updated[:half], number], axis=0).astype(BF16), top, NT)
    packed += dot(jnp.concatenate([updated[half:], number], axis=0).astype(BF16), bottom, NT)
    for s in range(shards):
        outgoing[s] = packed[:, s * 2 * SLOTS : (s + 1) * 2 * SLOTS].astype(BF16)


def main_kernel(target_payload, source_payload, relation, source, state, ids, q_high, q_low, rel_in, shard, changed,
                new_source, new_state, new_target, new_target_state, g_high, g_low, outgoing):
    width, rows = source.shape
    packed = target_payload[...].astype(jnp.int32)
    target = decoded(packed[:width], packed[width : width + 1])
    tail = packed[width : width + TAIL].astype(F32)
    target_state = (tail[1:2] + tail[2:3] * (1.0 / SCALE_UNIT)) * (1.0 / SCALE_UNIT)
    packed = source_payload[...].astype(jnp.int32)
    tail = packed[width : width + TAIL]
    behind = jnp.concatenate(halves(decoded(packed[:width], tail[0:1])), axis=0)
    relation3 = relation_parts(relation[...])
    parts = jnp.concatenate(halves(target), axis=1)
    gradient = jnp.zeros(source.shape, F32)
    pieces = LIVE // rows
    for i in range(pieces):
        src, tgt, rel, block = [tail[1 + j * pieces + i : 2 + j * pieces + i] for j in range(4)]
        qh, ql, _ = queries(behind, relation3, src, rel)
        gh, gl = score_gradients(parts, qh, ql, tgt, block)
        gradient += target_gradient(qh, ql, gh, gl)
    target, sums = adagrad(target, target_state, gradient)
    new_target[...] = target
    new_target_state[...] = sums
    high, low = halves(target)
    parts = jnp.concatenate([high, low], axis=1)
    stack = jnp.concatenate([high, low], axis=0)
    gradient = jnp.zeros(source.shape, F32)
    for first in range(0, LIVE, CHUNK):
        at = pl.ds(first, CHUNK)
        gh, gl = score_gradients(parts, q_high[:, at], q_low[:, at], ids[1:2, at], ids[3:4, at])
        g_high[:, at] = gh
        g_low[:, at] = gl
        gradient += source_gradient(stack, gh, gl, rel_in[:, at], ids[0:1, at])
    updated, sums = adagrad(source[...], state[...], gradient)
    new_source[...] = updated
    new_state[...] = sums
    publish(updated, shard[...], changed[...], outgoing)


def last_target_kernel(target, state, q_high, q_low, g_high, g_low, new_target, new_state):
    gradient = jnp.zeros(target.shape, F32)
    for first in range(0, LIVE, CHUNK):
        at = pl.ds(first, CHUNK)
        gradient += target_gradient(q_high[:, at], q_low[:, at], g_high[:, at], g_low[:, at])
    new_target[...], new_state[...] = adagrad(target[...], state[...], gradient)


def serve_kernel(incoming, served):
    shards, packed_rows, lanes = incoming.shape
    half = served.shape[1] // 2
    rows = served.shape[2]
    lane = lax.broadcasted_iota(jnp.int32, (rows, lanes), 1)
    number = (lax.broadcasted_iota(jnp.int32, (rows, lanes), 0) + 1).astype(F32)
    for s in range(shards):
        block = incoming[s]
        index = block[half : half + 8].astype(F32)[:1]
        match = number == index
        top = jnp.logical_and(match, lane < SLOTS).astype(F32)
        bottom = jnp.logical_and(match, lane >= SLOTS).astype(F32)
        spread = dot(block, jnp.concatenate([top, bottom], axis=0).astype(BF16), NT)
        served[s] = jnp.concatenate([spread[:half, :rows], spread[:half, rows:]], axis=0).astype(BF16)


VMEM = pl.BlockSpec(memory_space=pltpu.VMEM)
SMEM = pl.BlockSpec(memory_space=pltpu.SMEM)


def call(kernel, outs, args, scalars=(), flops=10**9):
    return pl.pallas_call(
        kernel,
        out_shape=[jax.ShapeDtypeStruct(shape, kind) for shape, kind in outs],
        in_specs=[SMEM if i in scalars else VMEM for i in range(len(args))],
        out_specs=[VMEM] * len(outs),
        compiler_params=pltpu.CompilerParams(vmem_limit_bytes=40 * 2**20),
        cost_estimate=pl.CostEstimate(flops=flops, bytes_accessed=4 * 2**20, transcendentals=2**17),
    )(*args)


def from_behind(block, axis, distance):
    devices = range(lax.axis_size(axis))
    route = [((i - distance) % len(devices), i) for i in devices]
    return lax.ppermute(block, axis, route)


def on_device(
    source_rows,
    source_state,
    target_rows,
    target_state,
    relation_table,
    source_ids,
    target_ids,
    relation_ids,
    negative_block,
    edge_counts,
    serving_shard,
    changed_rows,
):
    source = jnp.swapaxes(source_rows[0, 0], 0, 1)
    target = jnp.swapaxes(target_rows[0, 0], 0, 1)
    source_sums, target_sums = source_state[0], target_state[0]
    src, tgt, rel = source_ids[0, 0], target_ids[0, 0], relation_ids[0, 0]
    negatives, counts = negative_block[0, 0], edge_counts[0, 0]
    width, rows = source.shape
    shards = lax.axis_size("serve")
    matrix, line = ((width, rows), F32), ((1, rows), F32)
    edge16, edge32, grad16 = ((width, LIVE), BF16), ((width, LIVE), F32), ((rows, LIVE), BF16)
    payload, ids8 = ((width + TAIL, rows), jnp.int16), ((8, LIVE), jnp.int32)

    target_out = call(encode_target_kernel, [payload], (target, target_sums))[0]
    near_target = from_behind(target_out, "dom", 1)
    far_target = from_behind(target_out, "dom", 2)
    source_out, ids, ids_next = call(
        encode_source_kernel, [payload, ids8, ids8],
        (source, src, tgt, rel, negatives, counts), (4, 5))
    near_source = from_behind(source_out, "dom", 1)
    q_high, q_low, relation = call(query_kernel, [edge16, edge16, edge32], (source, relation_table, ids))
    source, source_sums, q_high, q_low, relation = call(
        source_kernel, [matrix, line, edge16, edge16, edge32],
        (near_target, source, source_sums, relation_table, ids, ids_next, q_high, q_low, relation))
    source, source_sums, target, target_sums, g_high, g_low, outgoing = call(
        main_kernel, [matrix, line, matrix, line, grad16, grad16, ((shards, width // 2 + 8, 2 * SLOTS), BF16)],
        (far_target, near_source, relation_table, source, source_sums, ids_next, q_high, q_low, relation,
         serving_shard[0], changed_rows[0]))
    incoming = lax.all_to_all(outgoing, "serve", split_axis=0, concat_axis=0, tiled=True)
    target, target_sums = call(last_target_kernel, [matrix, line], (target, target_sums, q_high, q_low, g_high, g_low))
    served = call(serve_kernel, [((shards, width, rows), BF16)], (incoming,))[0]
    return (
        jnp.swapaxes(source, 0, 1)[None, None],
        source_sums[None],
        jnp.swapaxes(target, 0, 1)[None, None],
        target_sums[None],
        jnp.swapaxes(served, 1, 2)[None, None],
    )


def solution(mesh):
    return jax.shard_map(
        on_device,
        mesh=mesh,
        in_specs=(
            P("dom", "serve", None, None),
            P("dom", "serve", None),
            P("dom", "serve", None, None),
            P("dom", "serve", None),
            P(),
            P("dom", "serve", None, None, None),
            P("dom", "serve", None, None, None),
            P("dom", "serve", None, None, None),
            P("dom", "serve", None, None),
            P("dom", "serve", None, None),
            P("dom", "serve", None),
            P("dom", "serve", None),
        ),
        out_specs=(
            P("dom", "serve", None, None),
            P("dom", "serve", None),
            P("dom", "serve", None, None),
            P("dom", "serve", None),
            P("dom", "serve", None, None, None),
        ),
        check_vma=False,
    )
```

time: 67.8 us -> 52.1 us (0.77)
  waiting for transfers between devices: 31.3 us -> 18.1 us
  local copies, waits for them, and re-layouts: 3.2 us -> 1.72 us
  starting transfers between devices: 17.1 us -> 15.7 us
  Pallas kernels: 14.7 us -> 15.4 us
    ppermute x4 -> x3, waiting for transfers between devices: 31.3 us -> 13.5 us  [from_behind(): return lax.ppermute(block, axis, route)]
    all_to_all x1, waiting for transfers between devices: 0.01 us -> 4.62 us  [on_device(): lax.all_to_all(outgoing, 'serve', split_axis=0, concat_axis=0, tiled=True)]
    unnamed x28 -> x24, local copies, waits for them, and re-layouts: 3.2 us -> 1.72 us
    all_to_all x1, starting transfers between devices: 6.18 us -> 5.23 us  [on_device(): lax.all_to_all(outgoing, 'serve', split_axis=0, concat_axis=0, tiled=True)]
    pallas_call x6 -> x7, Pallas kernels: 14.7 us -> 15.4 us  [call(): pl.pallas_call(kernel, out_shape=[jax.ShapeDtypeStruct(shape, kind) for s...]
    ppermute x4 -> x3, starting transfers between devices: 11 us -> 10.5 us  [from_behind(): return lax.ppermute(block, axis, route)]
  transfers between devices with their start and end apart: 5 -> 4, of which waited for: 3 -> 3; matrix products, arithmetic and copies ran while one was open for 0% -> 0% of each run, Pallas kernels for 8% -> 13%
where the time goes in v1:
time: 52.1 us; the launch traced here: 51.7 us
  waiting for transfers between devices  18.1 us (35%)
  starting transfers between devices  15.7 us (30%)
  Pallas kernels  15.4 us (30%)
  local copies, waits for them, and re-layouts  1.72 us (3%)
  between operations  0.8 us (2%)
    pallas_call x7, Pallas kernels, call(): pl.pallas_call(kernel, out_shape=[jax.ShapeDtypeStruct(shape, kind) for s...  15.4 us
    ppermute x3, waiting for transfers between devices, from_behind(): return lax.ppermute(block, axis, route)  13.5 us
    ppermute x3, starting transfers between devices, from_behind(): return lax.ppermute(block, axis, route)  10.5 us
    all_to_all x1, starting transfers between devices, on_device(): lax.all_to_all(outgoing, 'serve', split_axis=0, concat_axis=0, tiled=True)  5.23 us
    all_to_all x1, waiting for transfers between devices, on_device(): lax.all_to_all(outgoing, 'serve', split_axis=0, concat_axis=0, tiled=True)  4.62 us
    unnamed x24, local copies, waits for them, and re-layouts  1.72 us
  transfers between devices with their start and end apart: 4, of which 3 were waited for; matrix products, arithmetic and copies ran while one was open for 0% of the time, Pallas kernels for 13%

profile of v1, /device:TPU:1, one launch (start us, length us, event | category | flops | bytes accessed | tf_op | source)
XLA Modules:
  0.0 51.7 jit_solution(5321186584754218194)
XLA Ops:
  0.6 0.0 copy-start
  0.6 1.0 %copy-done = f32[1,1,256,400]{2,3,1,0:T(8,128)S(1)} copy-done((f32[1,1,256,400]{2,3,1,0:T(8,128)S(1)}, f32[1,1,256,400]{2,3,1,0:T(8,128)}, u32[]{:S(2)}) %copy-start) | copy-done | bytes 409624
  1.6 0.0 copy-start.6
  1.6 0.7 %copy-done.6 = f32[1,1,256]{2,1,0:T(1,128)S(1)} copy-done((f32[1,1,256]{2,1,0:T(1,128)S(1)}, f32[1,1,256]{2,1,0:T(1,128)}, u32[]{:S(2)}) %copy-start.6) | copy-done | bytes 1048
  2.3 0.0 copy-start.1
  2.3 0.0 copy-start.3
  2.3 0.0 copy-start.4
  2.3 0.0 copy-start.5
  2.3 0.0 copy-start.7
  2.3 0.0 copy-start.8
  2.3 0.1 shard_map.155
  2.5 4.1 %collective-permute-start.2 = (s16[416,256]{1,0:T(8,128)(2,1)S(1)}, s16[416,256]{1,0:T(8,128)(2,1)S(1)}, u32[]{:S(2)}, u32[]{:S(2)}) collective-permute-start(s16[416,256]{1,0:T(8,128)(2,1)S(1)} %shard_map.155), channel_id=1, source_target_pairs={{508,0},{0,4},{4,8},{8,12},{12,16},{16,20},{20,24},{24,28},{28,32}... | collective-permute-start | bytes 638984 | tf_op jit(solution)/shard_map/ppermute | solution.py:290
  6.6 3.2 %collective-permute-start = (s16[416,256]{1,0:T(8,128)(2,1)S(1)}, s16[416,256]{1,0:T(8,128)(2,1)S(1)}, u32[]{:S(2)}, u32[]{:S(2)}) collective-permute-start(s16[416,256]{1,0:T(8,128)(2,1)S(1)} %shard_map.155), channel_id=1, source_target_pairs={{504,0},{508,4},{0,8},{4,12},{8,16},{12,20},{16,24},{20,28},{24,32... | collective-permute-start | bytes 638984 | tf_op jit(solution)/shard_map/ppermute | solution.py:290
  9.8 0.0 copy-done.1
  9.8 0.0 copy-done.3
  9.8 0.0 copy-done.4
  9.8 0.0 copy-done.5
  9.8 0.0 copy-done.7
  9.8 0.0 copy-done.8
  9.8 0.0 copy-start.2
  9.9 1.4 %shard_map.156 = (s16[416,256]{1,0:T(8,128)(2,1)S(1)}, s32[8,768]{1,0:T(8,128)S(1)}, s32[8,768]{1,0:T(8,128)S(1)}) custom-call(f32[400,256]{1,0:T(8,128)S(1)} %bitcast.27, s32[2,8,128]{2,1,0:T(8,128)S(1)} %bitcast.30, s32[2,8,128]{2,1,0:T(8,128)S(1)} %bitcast.31, s32[2,8,128]{2,1,0:T(8,128)S(1)} %bitcast.32, s32[2,8]{1,0:T(2,128)S(1)} %bitcast.34, ...), custom_call_target="tpu_custom_call" | custom-call | flops 1000000000 | bytes 4194304 | tf_op jit(solution)/shard_map/pallas_call | solution.py:277
  11.2 3.2 %collective-permute-start.1 = (s16[416,256]{1,0:T(8,128)(2,1)S(1)}, s16[416,256]{1,0:T(8,128)(2,1)S(1)}, u32[]{:S(2)}, u32[]{:S(2)}) collective-permute-start(s16[416,256]{1,0:T(8,128)(2,1)S(1)} %get-tuple-element.25), channel_id=1, source_target_pairs={{508,0},{0,4},{4,8},{8,12},{12,16},{16,20},{20,24},{24,28},{28,32}... | collective-permute-start | bytes 638984 | tf_op jit(solution)/shard_map/ppermute | solution.py:290
  14.4 0.0 copy-done.2
  14.4 0.0 copy-start.9
  14.4 0.7 %shard_map.157 = (bf16[400,768]{1,0:T(8,128)(2,1)S(1)}, bf16[400,768]{1,0:T(8,128)(2,1)S(1)}, f32[400,768]{1,0:T(8,128)S(1)}) custom-call(f32[400,256]{1,0:T(8,128)S(1)} %bitcast.28, f32[16,400]{1,0:T(8,128)S(1)} %copy-done.2, s32[8,768]{1,0:T(8,128)S(1)} %get-tuple-element.26.ids), custom_call_target="tpu_custom_call" | custom-call | flops 1000000000 | bytes 4194304 | tf_op jit(solution)/shard_map/pallas_call | solution.py:277
  15.1 9.3 %collective-permute-done.2.payload = s16[416,256]{1,0:T(8,128)(2,1)S(1)} collective-permute-done((s16[416,256]{1,0:T(8,128)(2,1)S(1)}, s16[416,256]{1,0:T(8,128)(2,1)S(1)}, u32[]{:S(2)}, u32[]{:S(2)}) %collective-permute-start.2) | collective-permute-done | bytes 213024 | tf_op jit(solution)/shard_map/ppermute | solution.py:290
  24.4 0.0 copy-done.9
  24.4 0.0 copy-start.10
  24.4 0.0 copy-start.11
  24.4 3.4 %shard_map.158 = (f32[400,256]{1,0:T(8,128)S(1)}, f32[1,256]{1,0:T(1,128)S(1)}, bf16[400,768]{1,0:T(8,128)(2,1)S(1)}, bf16[400,768]{1,0:T(8,128)(2,1)S(1)}, f32[400,768]{1,0:T(8,128)S(1)}) custom-call(s16[416,256]{1,0:T(8,128)(2,1)S(1)} %collective-permute-done.2.payload, f32[400,256]{1,0:T(8,128)S(1)} %bitcast.29, f32[1,256]{1,0:T(1,128)S(1)} %bitcast.36, ...), custom_call_target="tpu_custom_call" | custom-call | flops 1000000000 | bytes 4194304 | tf_op jit(solution)/shard_map/pallas_call | solution.py:277
  27.8 0.0 collective-permute-done.target_payload
  27.8 4.2 %collective-permute-done.1.source_payload = s16[416,256]{1,0:T(8,128)(2,1)S(1)} collective-permute-done((s16[416,256]{1,0:T(8,128)(2,1)S(1)}, s16[416,256]{1,0:T(8,128)(2,1)S(1)}, u32[]{:S(2)}, u32[]{:S(2)}) %collective-permute-start.1) | collective-permute-done | bytes 213024 | tf_op jit(solution)/shard_map/ppermute | solution.py:290
  32.0 0.0 copy-done.10
  32.0 0.0 copy-done.11
  32.0 7.0 %shard_map.159 = (f32[400,256]{1,0:T(8,128)}, f32[1,256]{1,0:T(1,128)}, f32[400,256]{1,0:T(8,128)S(1)}, f32[1,256]{1,0:T(1,128)S(1)}, bf16[256,768]{1,0:T(8,128)...) custom-call(s16[416,256]{1,0:T(8,128)(2,1)S(1)} %collective-permute-done.target_payload, ...), custom_call_target="tpu_custom_call" | custom-call | flops 1000000000 | bytes 4194304 | tf_op jit(solution)/shard_map/pallas_call | solution.py:277
  39.1 5.2 %all-to-all-start = ((bf16[4,208,128]{2,1,0:T(8,128)(2,1)}), bf16[4,208,128]{2,1,0:T(8,128)(2,1)S(1)}, u32[]{:S(2)}, u32[]{:S(2)}) async-start(bf16[4,208,128]{2,1,0:T(8,128)(2,1)} %get-tuple-element.44), calls=%async_computation | async-start | bytes 425984 | tf_op jit(solution)/shard_map/all_to_all | solution.py:333
  44.3 1.5 %shard_map.160 = (f32[400,256]{1,0:T(8,128)}, f32[1,256]{1,0:T(1,128)}) custom-call(f32[400,256]{1,0:T(8,128)S(1)} %get-tuple-element.38.target, f32[1,256]{1,0:T(1,128)S(1)} %get-tuple-element.39.state, bf16[400,768]{1,0:T(8,128)(2,1)S(1)} %get-tuple-element.33.q_high, bf16[400,768]{1,0:T(8,128)(2,1)S(1)} %get-tuple-element.34.q_low, ...), custom_call_target="tpu_custom_call" | custom-call | flops 1000000000 | bytes 4194304 | tf_op jit(solution)/shard_map/pallas_call | solution.py:277
  45.8 4.6 %all-to-all-done.incoming = bf16[4,208,128]{2,1,0:T(8,128)(2,1)S(1)} async-done(((bf16[4,208,128]{2,1,0:T(8,128)(2,1)}), bf16[4,208,128]{2,1,0:T(8,128)(2,1)S(1)}, u32[]{:S(2)}, u32[]{:S(2)}) %all-to-all-start) | async-done | bytes 213024 | tf_op jit(solution)/shard_map/all_to_all | solution.py:333
  50.5 1.3 %shard_map.161 = bf16[4,400,256]{2,1,0:T(8,128)(2,1)} custom-call(bf16[4,208,128]{2,1,0:T(8,128)(2,1)S(1)} %all-to-all-done.incoming), custom_call_target="tpu_custom_call" | custom-call | flops 1000000000 | bytes 4194304 | tf_op jit(solution)/shard_map/pallas_call | solution.py:277
Async XLA Ops:
  0.6 1.0 %copy-start = (f32[1,1,256,400]{2,3,1,0:T(8,128)S(1)}, f32[1,1,256,400]{2,3,1,0:T(8,128)}, u32[]{:S(2)}) copy-start(f32[1,1,256,400]{2,3,1,0:T(8,128)} %param.14) | copy-start | bytes 1228804
  1.6 0.7 %copy-start.6 = (f32[1,1,256]{2,1,0:T(1,128)S(1)}, f32[1,1,256]{2,1,0:T(1,128)}, u32[]{:S(2)}) copy-start(f32[1,1,256]{2,1,0:T(1,128)} %param.15) | copy-start | bytes 3076
  2.3 7.5 %copy-start.1 = (f32[1,1,256,400]{2,3,1,0:T(8,128)S(1)}, f32[1,1,256,400]{2,3,1,0:T(8,128)}, u32[]{:S(2)}) copy-start(f32[1,1,256,400]{2,3,1,0:T(8,128)} %param.12) | copy-start | bytes 1228804
  2.3 7.5 %copy-start.3 = (s32[1,1,2,8,128]{4,3,2,1,0:T(8,128)S(1)}, s32[1,1,2,8,128]{4,3,2,1,0:T(8,128)}, u32[]{:S(2)}) copy-start(s32[1,1,2,8,128]{4,3,2,1,0:T(8,128)} %param.17) | copy-start | bytes 24580
  2.3 7.5 %copy-start.4 = (s32[1,1,2,8,128]{4,3,2,1,0:T(8,128)S(1)}, s32[1,1,2,8,128]{4,3,2,1,0:T(8,128)}, u32[]{:S(2)}) copy-start(s32[1,1,2,8,128]{4,3,2,1,0:T(8,128)} %param.18) | copy-start | bytes 24580
  2.3 7.5 %copy-start.5 = (s32[1,1,2,8,128]{4,3,2,1,0:T(8,128)S(1)}, s32[1,1,2,8,128]{4,3,2,1,0:T(8,128)}, u32[]{:S(2)}) copy-start(s32[1,1,2,8,128]{4,3,2,1,0:T(8,128)} %param.19) | copy-start | bytes 24580
  2.3 7.5 %copy-start.7 = (s32[1,1,2,8]{3,2,1,0:T(2,128)S(1)}, s32[1,1,2,8]{3,2,1,0:T(2,128)}, u32[]{:S(2)}) copy-start(s32[1,1,2,8]{3,2,1,0:T(2,128)} %param.20) | copy-start | bytes 196
  2.3 7.5 %copy-start.8 = (s32[1,1,2,8]{3,2,1,0:T(2,128)S(1)}, s32[1,1,2,8]{3,2,1,0:T(2,128)}, u32[]{:S(2)}) copy-start(s32[1,1,2,8]{3,2,1,0:T(2,128)} %param.21) | copy-start | bytes 196
  2.5 21.9 %collective-permute-start.2 = (s16[416,256]{1,0:T(8,128)(2,1)S(1)}, s16[416,256]{1,0:T(8,128)(2,1)S(1)}, u32[]{:S(2)}, u32[]{:S(2)}) collective-permute-start(s16[416,256]{1,0:T(8,128)(2,1)S(1)} %shard_map.155), channel_id=1, source_target_pairs={{508,0},{0,4},{4,8},{8,12},{12,16},{16,20},{20,24},{24,28},{28,32}... | collective-permute-start | bytes 638984 | tf_op jit(solution)/shard_map/ppermute | solution.py:290
  6.6 21.3 %collective-permute-start = (s16[416,256]{1,0:T(8,128)(2,1)S(1)}, s16[416,256]{1,0:T(8,128)(2,1)S(1)}, u32[]{:S(2)}, u32[]{:S(2)}) collective-permute-start(s16[416,256]{1,0:T(8,128)(2,1)S(1)} %shard_map.155), channel_id=1, source_target_pairs={{504,0},{508,4},{0,8},{4,12},{8,16},{12,20},{16,24},{20,28},{24,32... | collective-permute-start | bytes 638984 | tf_op jit(solution)/shard_map/ppermute | solution.py:290
  9.8 4.6 %copy-start.2 = (f32[16,400]{1,0:T(8,128)S(1)}, f32[16,400]{1,0:T(8,128)}, u32[]{:S(2)}) copy-start(f32[16,400]{1,0:T(8,128)} %relation.5) | copy-start | bytes 76804
  11.2 20.8 %collective-permute-start.1 = (s16[416,256]{1,0:T(8,128)(2,1)S(1)}, s16[416,256]{1,0:T(8,128)(2,1)S(1)}, u32[]{:S(2)}, u32[]{:S(2)}) collective-permute-start(s16[416,256]{1,0:T(8,128)(2,1)S(1)} %get-tuple-element.25), channel_id=1, source_target_pairs={{508,0},{0,4},{4,8},{8,12},{12,16},{16,20},{20,24},{24,28},{28,32}... | collective-permute-start | bytes 638984 | tf_op jit(solution)/shard_map/ppermute | solution.py:290
  14.4 10.0 %copy-start.9 = (f32[1,1,256]{2,1,0:T(1,128)S(1)}, f32[1,1,256]{2,1,0:T(1,128)}, u32[]{:S(2)}) copy-start(f32[1,1,256]{2,1,0:T(1,128)} %param.13) | copy-start | bytes 3076
  24.4 7.6 %copy-start.10 = (s32[1,1,256]{2,1,0:T(1,128)S(1)}, s32[1,1,256]{2,1,0:T(1,128)}, u32[]{:S(2)}) copy-start(s32[1,1,256]{2,1,0:T(1,128)} %param.22) | copy-start | bytes 3076
  24.4 7.6 %copy-start.11 = (s32[1,1,256]{2,1,0:T(1,128)S(1)}, s32[1,1,256]{2,1,0:T(1,128)}, u32[]{:S(2)}) copy-start(s32[1,1,256]{2,1,0:T(1,128)} %param.23) | copy-start | bytes 3076
  39.1 11.4 %all-to-all-start = ((bf16[4,208,128]{2,1,0:T(8,128)(2,1)}), bf16[4,208,128]{2,1,0:T(8,128)(2,1)S(1)}, u32[]{:S(2)}, u32[]{:S(2)}) async-start(bf16[4,208,128]{2,1,0:T(8,128)(2,1)} %get-tuple-element.44), calls=%async_computation | async-start | bytes 425984 | tf_op jit(solution)/shard_map/all_to_all | solution.py:333

commit v2 on v1

--- a/solution.py
+++ b/solution.py
@@ -15,7 +15,7 @@
 NT = ((1,), (1,))
 TN = ((0,), (0,))
 LANES = 128
-CHUNK = 256
+CHUNK = 768
 LIVE = 768
 SCALE_UNIT = 16384.0
 CODE_MAX = 32767.0
@@ -89,20 +89,18 @@
 
 
 def queries(source_stack, relation3, src, rel):
-    width = source_stack.shape[0] // 2
     relations = relation3.shape[0] // 3
-    both = dot(source_stack, one_hot(src, source_stack.shape[1]), NN)
+    rows = one_hot(src, source_stack.shape[1] // 2)
     pick = one_hot(rel, relations)
     relation = dot(relation3, jnp.concatenate([pick, pick, pick], axis=0), TN)
-    qh, ql = halves((both[:width] + both[width:]) * relation)
+    qh, ql = halves(dot(source_stack, jnp.concatenate([rows, rows], axis=0), NN) * relation)
     return qh, ql, relation
 
 
 def score_gradients(target_parts, qh, ql, tgt, block):
-    rows = target_parts.shape[1] // 2
+    rows = target_parts.shape[0]
     lanes = tgt.shape[1]
-    both = dot(target_parts, qh, TN)
-    scores = both[:rows] + both[rows:] + dot(target_parts[:, :rows], ql, TN)
+    scores = dot(target_parts, jnp.concatenate([qh, qh, ql], axis=0), NN)
     hit = lax.broadcasted_iota(jnp.int32, (rows, lanes), 0) == tgt
     positive = jnp.sum(jnp.where(hit, scores, 0.0), axis=0, keepdims=True)
     dpos = -sigmoid(-positive)
@@ -113,6 +111,10 @@
     return halves(spread + jnp.where(hit, dpos, 0.0))
 
 
+def row_major(high, low):
+    return jnp.concatenate([high.T, low.T, high.T], axis=1)
+
+
 def adagrad(weights, state, gradient):
     new_state = state + jnp.sum(gradient * gradient, axis=0, keepdims=True) * (1.0 / gradient.shape[0])
     scale = LEARN_RATE / (jnp.sqrt(new_state) + EPSILON)
@@ -120,48 +122,61 @@
 
 
 def target_gradient(qh, ql, gh, gl):
-    width = qh.shape[0]
-    both = dot(jnp.concatenate([qh, ql], axis=0), gh, NT)
-    return both[:width] + both[width:] + dot(qh, gl, NT)
+    return dot(jnp.concatenate([qh, ql, qh], axis=1), jnp.concatenate([gh, gh, gl], axis=1), NT)
 
 
 def source_gradient(target_stack, gh, gl, relation, src):
-    width = relation.shape[0]
-    both = dot(target_stack, gh, NN)
-    flow = (both[:width] + both[width:] + dot(target_stack[:width], gl, NN)) * relation
-    fh, fl = halves(flow)
-    both = dot(jnp.concatenate([fh, fl], axis=0), one_hot(src, gh.shape[0]), NT)
-    return both[:width] + both[width:]
-
-
-def encode_target_kernel(target, state, payload):
+    flow = dot(target_stack, jnp.concatenate([gh, gh, gl], axis=0), NN) * relation
+    rows = one_hot(src, gh.shape[0])
+    return dot(jnp.concatenate(halves(flow), axis=1), jnp.concatenate([rows, rows], axis=1), NT)
+
+
+def encode_target_kernel(target, payload):
     codes, unit = coded(target[...])
-    scaled = state[...] * SCALE_UNIT
-    whole = jnp.floor(scaled)
-    part = jnp.floor((scaled - whole) * SCALE_UNIT + 0.5)
-    tail = pick_rows(
-        range(3), [unit, whole.astype(jnp.int32), part.astype(jnp.int32)], (TAIL, target.shape[1]))
+    tail = pick_rows((0,), [unit], (TAIL, target.shape[1]))
     payload[...] = jnp.concatenate([codes, tail], axis=0).astype(jnp.int16)
 
 
-def encode_source_kernel(source, src_ref, tgt_ref, rel_ref, nb_ref, count_ref, payload, ids_now, ids_next):
+def encode_source_kernel(source, src, tgt, rel, nb_ref, count_ref, near, state, payload, far, ids_now):
+    width, rows = source.shape
     codes, unit = coded(source[...])
-    rows = source.shape[1]
-    ids = compact(0, src_ref, tgt_ref, rel_ref, nb_ref, count_ref)
+    ids = compact(0, src, tgt, rel, nb_ref, count_ref)
     ids_now[...] = pick_rows(range(4), ids, ids_now.shape)
     pieces = [i[:, at : at + rows] for i in ids for at in range(0, LIVE, rows)]
     tail = pick_rows(range(TAIL), [unit] + pieces, (TAIL, rows))
     payload[...] = jnp.concatenate([codes, tail], axis=0).astype(jnp.int16)
-    ids = compact(1, src_ref, tgt_ref, rel_ref, nb_ref, count_ref)
-    ids_next[...] = pick_rows(range(4), ids, ids_next.shape)
-
-
-def query_kernel(source, relation, ids, q_high, q_low, rel_out):
-    stack = jnp.concatenate(halves(source[...]), axis=0)
+    scaled = state[...] * SCALE_UNIT
+    whole = jnp.floor(scaled)
+    part = jnp.floor((scaled - whole) * SCALE_UNIT + 0.5)
+    unit = near[width : width + TAIL].astype(jnp.int32)[:1]
+    tail = pick_rows(range(3), [unit, whole.astype(jnp.int32), part.astype(jnp.int32)], (TAIL, rows))
+    far[:width] = near[:width]
+    far[width:] = tail.astype(jnp.int16)
+
+
+def query_kernel(source, relation, ids, src_ref, tgt_ref, rel_ref, nb_ref, count_ref, shard, changed,
+                 q_high, q_low, rel_out, ids_next, top, bottom):
+    stack = jnp.concatenate(halves(source[...]), axis=1)
     relation3 = relation_parts(relation[...])
     for first in range(0, LIVE, CHUNK):
         at = pl.ds(first, CHUNK)
         q_high[:, at], q_low[:, at], rel_out[:, at] = queries(stack, relation3, ids[0:1, at], ids[2:3, at])
+    ids_next[...] = pick_rows(range(4), compact(1, src_ref, tgt_ref, rel_ref, nb_ref, count_ref), ids_next.shape)
+    slots(shard[...], changed[...], top, bottom)
+
+
+def behind_kernel(payload, relation, q_high, q_low, ids):
+    width, rows = payload.shape[0] - TAIL, payload.shape[1]
+    packed = payload[...].astype(jnp.int32)
+    tail = packed[width:]
+    stack = jnp.concatenate(halves(decoded(packed[:width], tail[0:1])), axis=1)
+    relation3 = relation_parts(relation[...])
+    pieces = LIVE // rows
+    for i in range(pieces):
+        at = pl.ds(i * rows, rows)
+        src, tgt, rel, block = [tail[1 + j * pieces + i : 2 + j * pieces + i] for j in range(4)]
+        q_high[:, at], q_low[:, at], _ = queries(stack, relation3, src, rel)
+        ids[:, at] = pick_rows((1, 3), (tgt, block), (8, rows))
 
 
 def source_kernel(payload, source, state, relation, ids, ids_next, q_high, q_low, rel_in,
@@ -169,8 +184,8 @@
     width = source.shape[0]
     packed = payload[...].astype(jnp.int32)
     high, low = halves(decoded(packed[:width], packed[width : width + 1]))
-    parts = jnp.concatenate([high, low], axis=1)
-    stack = jnp.concatenate([high, low], axis=0)
+    stack = jnp.concatenate([high, low, high], axis=1)
+    parts = row_major(high, low)
     gradient = jnp.zeros(source.shape, F32)
     for first in range(0, LIVE, CHUNK):
         at = pl.ds(first, CHUNK)
@@ -179,7 +194,7 @@
     updated, sums = adagrad(source[...], state[...], gradient)
     new_source[...] = updated
     new_state[...] = sums
-    stack = jnp.concatenate(halves(updated), axis=0)
+    stack = jnp.concatenate(halves(updated), axis=1)
     relation3 = relation_parts(relation[...])
     for first in range(0, LIVE, CHUNK):
         at = pl.ds(first, CHUNK)
@@ -187,51 +202,50 @@
             stack, relation3, ids_next[0:1, at], ids_next[2:3, at])
 
 
-def publish(updated, shard, changed, outgoing):
+def slots(shard, changed, top, bottom):
+    rows = shard.shape[1]
+    is_row = lax.broadcasted_iota(jnp.int32, (8, rows), 0)
+    mine = jnp.logical_and(is_row == shard, changed == 1).astype(F32)
+    before = lax.broadcasted_iota(jnp.int32, (rows, rows), 0) < lax.broadcasted_iota(jnp.int32, (rows, rows), 1)
+    rank = dot(mine.astype(BF16), before.astype(F32).astype(BF16), NN)
+    slot = jnp.sum(mine * rank, axis=0, keepdims=True).astype(jnp.int32)
+    code = jnp.where(changed == 1, shard * (2 * SLOTS) + slot, -2 * SLOTS)
+    top[...] = one_hot(code, top.shape[0])
+    bottom[...] = one_hot(code + SLOTS, bottom.shape[0])
+
+
+def publish(updated, top, bottom, outgoing):
     width, rows = updated.shape
     half = width // 2
-    is_row = lax.broadcasted_iota(jnp.int32, (8, rows), 0)
-    mine = jnp.logical_and(is_row == shard, changed == 1).astype(F32)
-    before = (lax.broadcasted_iota(jnp.int32, (rows, rows), 0) < lax.broadcasted_iota(jnp.int32, (rows, rows), 1))
-    rank = dot(mine.astype(BF16), before.astype(F32).astype(BF16), NN)
-    slot = jnp.sum(mine * rank, axis=0, keepdims=True).astype(jnp.int32)
-    code = jnp.where(changed == 1, shard * (2 * SLOTS) + slot, -1)
-    shards = outgoing.shape[0]
-    place = lax.broadcasted_iota(jnp.int32, (shards * 2 * SLOTS, rows), 0)
-    top = (place == code).astype(F32).astype(BF16)
-    bottom = jnp.logical_and(place == code + SLOTS, code >= 0).astype(F32).astype(BF16)
     number = (lax.broadcasted_iota(jnp.int32, (8, rows), 1) + 1).astype(F32)
-    packed = dot(jnp.concatenate([updated[:half], number], axis=0).astype(BF16), top, NT)
-    packed += dot(jnp.concatenate([updated[half:], number], axis=0).astype(BF16), bottom, NT)
-    for s in range(shards):
-        outgoing[s] = packed[:, s * 2 * SLOTS : (s + 1) * 2 * SLOTS].astype(BF16)
-
-
-def main_kernel(target_payload, source_payload, relation, source, state, ids, q_high, q_low, rel_in, shard, changed,
+    packed = dot(
+        jnp.concatenate([jnp.concatenate([updated[:half], number], axis=0).astype(BF16),
+                         jnp.concatenate([updated[half:], number], axis=0).astype(BF16)], axis=1),
+        jnp.concatenate([top, bottom], axis=1), NT).astype(BF16)
+    for s in range(outgoing.shape[0]):
+        outgoing[s] = packed[:, s * 2 * SLOTS : (s + 1) * 2 * SLOTS]
+
+
+def main_kernel(payload, behind_high, behind_low, behind_ids, source, state, ids, q_high, q_low, rel_in, top, bottom,
                 new_source, new_state, new_target, new_target_state, g_high, g_low, outgoing):
     width, rows = source.shape
-    packed = target_payload[...].astype(jnp.int32)
+    packed = payload[...].astype(jnp.int32)
     target = decoded(packed[:width], packed[width : width + 1])
-    tail = packed[width : width + TAIL].astype(F32)
+    tail = packed[width:].astype(F32)
     target_state = (tail[1:2] + tail[2:3] * (1.0 / SCALE_UNIT)) * (1.0 / SCALE_UNIT)
-    packed = source_payload[...].astype(jnp.int32)
-    tail = packed[width : width + TAIL]
-    behind = jnp.concatenate(halves(decoded(packed[:width], tail[0:1])), axis=0)
-    relation3 = relation_parts(relation[...])
-    parts = jnp.concatenate(halves(target), axis=1)
+    parts = row_major(*halves(target))
     gradient = jnp.zeros(source.shape, F32)
-    pieces = LIVE // rows
-    for i in range(pieces):
-        src, tgt, rel, block = [tail[1 + j * pieces + i : 2 + j * pieces + i] for j in range(4)]
-        qh, ql, _ = queries(behind, relation3, src, rel)
-        gh, gl = score_gradients(parts, qh, ql, tgt, block)
+    for first in range(0, LIVE, CHUNK):
+        at = pl.ds(first, CHUNK)
+        qh, ql = behind_high[:, at], behind_low[:, at]
+        gh, gl = score_gradients(parts, qh, ql, behind_ids[1:2, at], behind_ids[3:4, at])
         gradient += target_gradient(qh, ql, gh, gl)
     target, sums = adagrad(target, target_state, gradient)
     new_target[...] = target
     new_target_state[...] = sums
     high, low = halves(target)
-    parts = jnp.concatenate([high, low], axis=1)
-    stack = jnp.concatenate([high, low], axis=0)
+    stack = jnp.concatenate([high, low, high], axis=1)
+    parts = row_major(high, low)
     gradient = jnp.zeros(source.shape, F32)
     for first in range(0, LIVE, CHUNK):
         at = pl.ds(first, CHUNK)
@@ -242,7 +256,7 @@
     updated, sums = adagrad(source[...], state[...], gradient)
     new_source[...] = updated
     new_state[...] = sums
-    publish(updated, shard[...], changed[...], outgoing)
+    publish(updated, top[...], bottom[...], outgoing)
 
 
 def last_target_kernel(target, state, q_high, q_low, g_high, g_low, new_target, new_state):
@@ -280,7 +294,7 @@
         in_specs=[SMEM if i in scalars else VMEM for i in range(len(args))],
         out_specs=[VMEM] * len(outs),
         compiler_params=pltpu.CompilerParams(vmem_limit_bytes=40 * 2**20),
-        cost_estimate=pl.CostEstimate(flops=flops, bytes_accessed=4 * 2**20, transcendentals=2**17),
+        cost_estimate=pl.CostEstimate(flops=flops, bytes_accessed=2**16, transcendentals=0),
     )(*args)
 
 
@@ -313,23 +327,28 @@
     shards = lax.axis_size("serve")
     matrix, line = ((width, rows), F32), ((1, rows), F32)
     edge16, edge32, grad16 = ((width, LIVE), BF16), ((width, LIVE), F32), ((rows, LIVE), BF16)
+    shard, changed = serving_shard[0], changed_rows[0]
     payload, ids8 = ((width + TAIL, rows), jnp.int16), ((8, LIVE), jnp.int32)
-
-    target_out = call(encode_target_kernel, [payload], (target, target_sums))[0]
-    near_target = from_behind(target_out, "dom", 1)
-    far_target = from_behind(target_out, "dom", 2)
-    source_out, ids, ids_next = call(
-        encode_source_kernel, [payload, ids8, ids8],
-        (source, src, tgt, rel, negatives, counts), (4, 5))
+    places = ((shards * 2 * SLOTS, rows), BF16)
+
+    near_out = call(encode_target_kernel, [payload], (target,))[0]
+    source_out, far_out, ids = call(
+        encode_source_kernel, [payload, payload, ids8],
+        (source, src, tgt, rel, negatives, counts, near_out, target_sums), (4, 5))
+    near_target = from_behind(near_out, "dom", 1)
     near_source = from_behind(source_out, "dom", 1)
-    q_high, q_low, relation = call(query_kernel, [edge16, edge16, edge32], (source, relation_table, ids))
+    far_target = from_behind(far_out, "dom", 2)
+    q_high, q_low, relation, ids_next, top, bottom = call(
+        query_kernel, [edge16, edge16, edge32, ids8, places, places],
+        (source, relation_table, ids, src, tgt, rel, negatives, counts, shard, changed), (6, 7))
     source, source_sums, q_high, q_low, relation = call(
         source_kernel, [matrix, line, edge16, edge16, edge32],
-        (near_target, source, source_sums, relation_table, ids, ids_next, q_high, q_low, relation))
+        (near_target, source, source_sums, relation_table, ids, ids_next, q_high, q_low, relation), flops=8 * 10**9)
+    behind_high, behind_low, behind_ids = call(
+        behind_kernel, [edge16, edge16, ids8], (near_source, relation_table), flops=10**6)
     source, source_sums, target, target_sums, g_high, g_low, outgoing = call(
         main_kernel, [matrix, line, matrix, line, grad16, grad16, ((shards, width // 2 + 8, 2 * SLOTS), BF16)],
-        (far_target, near_source, relation_table, source, source_sums, ids_next, q_high, q_low, relation,
-         serving_shard[0], changed_rows[0]))
+        (far_target, behind_high, behind_low, behind_ids, source, source_sums, ids_next, q_high, q_low, relation, top, bottom))
     incoming = lax.all_to_all(outgoing, "serve", split_axis=0, concat_axis=0, tiled=True)
     target, target_sums = call(last_target_kernel, [matrix, line], (target, target_sums, q_high, q_low, g_high, g_low))
     served = call(serve_kernel, [((shards, width, rows), BF16)], (incoming,))[0]

time: 52.1 us -> 50.5 us (0.969)
  waiting for transfers between devices: 18.1 us -> 16.1 us
  starting transfers between devices: 15.7 us -> 16.9 us
  local copies, waits for them, and re-layouts: 1.72 us -> 1.05 us
    ppermute x3, waiting for transfers between devices: 13.5 us -> 11.5 us  [from_behind(): return lax.ppermute(block, axis, route)]
    all_to_all x1, starting transfers between devices: 5.23 us -> 6.47 us  [on_device(): lax.all_to_all(outgoing, 'serve', split_axis=0, concat_axis=0, tiled=True)]
    unnamed x24, local copies, waits for them, and re-layouts: 1.72 us -> 1.05 us
    pallas_call x7 -> x8, Pallas kernels: 15.4 us -> 15.3 us  [call(): pl.pallas_call(kernel, out_shape=[jax.ShapeDtypeStruct(shape, kind) for s...]
  transfers between devices with their start and end apart: 4 -> 4, of which waited for: 3 -> 3; matrix products, arithmetic and copies ran while one was open for 0% -> 0% of each run, Pallas kernels for 13% -> 16%
where the time goes in v2:
time: 50.5 us; the launch traced here: 50.2 us
  starting transfers between devices  16.9 us (33%)
  waiting for transfers between devices  16.1 us (32%)
  Pallas kernels  15.3 us (30%)
  local copies, waits for them, and re-layouts  1.05 us (2%)
  between operations  0.85 us (2%)
    pallas_call x8, Pallas kernels, call(): pl.pallas_call(kernel, out_shape=[jax.ShapeDtypeStruct(shape, kind) for s...  15.3 us
    ppermute x3, waiting for transfers between devices, from_behind(): return lax.ppermute(block, axis, route)  11.5 us
    ppermute x3, starting transfers between devices, from_behind(): return lax.ppermute(block, axis, route)  10.5 us
    all_to_all x1, starting transfers between devices, on_device(): lax.all_to_all(outgoing, 'serve', split_axis=0, concat_axis=0, tiled=True)  6.47 us
    all_to_all x1, waiting for transfers between devices, on_device(): lax.all_to_all(outgoing, 'serve', split_axis=0, concat_axis=0, tiled=True)  4.6 us
    unnamed x24, local copies, waits for them, and re-layouts  1.05 us
  transfers between devices with their start and end apart: 4, of which 3 were waited for; matrix products, arithmetic and copies ran while one was open for 0% of the time, Pallas kernels for 16%

profile of v2, /device:TPU:1, one launch (start us, length us, event | category | flops | bytes accessed | tf_op | source)
XLA Modules:
  0.0 50.2 jit_solution(4679273298278216515)
XLA Ops:
  0.6 0.0 copy-start.1
  0.6 1.0 %copy-done.1 = f32[1,1,256,400]{2,3,1,0:T(8,128)S(1)} copy-done((f32[1,1,256,400]{2,3,1,0:T(8,128)S(1)}, f32[1,1,256,400]{2,3,1,0:T(8,128)}, u32[]{:S(2)}) %copy-start.1) | copy-done | bytes 409624
  1.6 0.0 copy-start.2
  1.6 0.0 copy-start.3
  1.6 0.0 copy-start.4
  1.6 0.0 copy-start.5
  1.6 0.0 copy-start.6
  1.7 0.0 copy-start.7
  1.7 0.0 copy-start.8
  1.7 0.1 shard_map.155.near
  1.8 4.1 %collective-permute-start.2 = (s16[416,256]{1,0:T(8,128)(2,1)S(1)}, s16[416,256]{1,0:T(8,128)(2,1)S(1)}, u32[]{:S(2)}, u32[]{:S(2)}) collective-permute-start(s16[416,256]{1,0:T(8,128)(2,1)S(1)} %shard_map.155.near), channel_id=1, source_target_pairs={{508,0},{0,4},{4,8},{8,12},{12,16},{16,20},{20,24},{24,28},{28,32}... | collective-permute-start | bytes 638984 | tf_op jit(solution)/shard_map/ppermute | solution.py:304
  5.9 0.0 copy-done.2
  5.9 0.0 copy-done.3
  5.9 0.0 copy-done.4
  5.9 0.0 copy-done.5
  5.9 0.0 copy-done.6
  6.0 0.0 copy-done.7
  6.0 0.0 copy-done.8
  6.0 0.0 copy-start
  6.0 0.0 copy-start.9
  6.0 0.0 copy-start.10
  6.0 1.0 %shard_map.156 = (s16[416,256]{1,0:T(8,128)(2,1)S(1)}, s16[416,256]{1,0:T(8,128)(2,1)S(1)}, s32[8,768]{1,0:T(8,128)S(1)}) custom-call(f32[400,256]{1,0:T(8,128)S(1)} %bitcast.27, s32[2,8,128]{2,1,0:T(8,128)S(1)} %bitcast.30, s32[2,8,128]{2,1,0:T(8,128)S(1)} %bitcast.32, s32[2,8,128]{2,1,0:T(8,128)S(1)} %bitcast.34, s32[2,8]{1,0:T(2,128)S(1)} %bitcast.37, ...), custom_call_target="tpu_custom_call" | custom-call | flops 1000000000 | bytes 65536 | tf_op jit(solution)/shard_map/pallas_call | solution.py:291
  7.0 3.2 %collective-permute-start.1 = (s16[416,256]{1,0:T(8,128)(2,1)S(1)}, s16[416,256]{1,0:T(8,128)(2,1)S(1)}, u32[]{:S(2)}, u32[]{:S(2)}) collective-permute-start(s16[416,256]{1,0:T(8,128)(2,1)S(1)} %get-tuple-element.32), channel_id=1, source_target_pairs={{508,0},{0,4},{4,8},{8,12},{12,16},{16,20},{20,24},{24,28},{28,32}... | collective-permute-start | bytes 638984 | tf_op jit(solution)/shard_map/ppermute | solution.py:304
  10.2 3.2 %collective-permute-start = (s16[416,256]{1,0:T(8,128)(2,1)S(1)}, s16[416,256]{1,0:T(8,128)(2,1)S(1)}, u32[]{:S(2)}, u32[]{:S(2)}) collective-permute-start(s16[416,256]{1,0:T(8,128)(2,1)S(1)} %get-tuple-element.31), channel_id=1, source_target_pairs={{504,0},{508,4},{0,8},{4,12},{8,16},{12,20},{16,24},{20,28},{24,32... | collective-permute-start | bytes 638984 | tf_op jit(solution)/shard_map/ppermute | solution.py:304
  13.4 0.0 copy-done
  13.4 0.0 copy-done.9
  13.4 0.0 copy-done.10
  13.4 0.0 copy-start.11
  13.4 1.7 %shard_map.158 = (bf16[400,768]{1,0:T(8,128)(2,1)S(1)}, bf16[400,768]{1,0:T(8,128)(2,1)S(1)}, f32[400,768]{1,0:T(8,128)S(1)}, s32[8,768]{1,0:T(8,128)S(1)}, bf16...) custom-call(f32[400,256]{1,0:T(8,128)S(1)} %bitcast.28, f32[16,400]{1,0:T(8,128)S(1)} %copy-done, ...), custom_call_target="tpu_custom_call" | custom-call | flops 1000000000 | bytes 65536 | tf_op jit(solution)/shard_map/pallas_call | solution.py:291
  15.2 7.1 %collective-permute-done.2.payload = s16[416,256]{1,0:T(8,128)(2,1)S(1)} collective-permute-done((s16[416,256]{1,0:T(8,128)(2,1)S(1)}, s16[416,256]{1,0:T(8,128)(2,1)S(1)}, u32[]{:S(2)}, u32[]{:S(2)}) %collective-permute-start.2) | collective-permute-done | bytes 213024 | tf_op jit(solution)/shard_map/ppermute | solution.py:304
  22.2 0.0 copy-done.11
  22.2 3.1 %shard_map.159 = (f32[400,256]{1,0:T(8,128)S(1)}, f32[1,256]{1,0:T(1,128)S(1)}, bf16[400,768]{1,0:T(8,128)(2,1)S(1)}, bf16[400,768]{1,0:T(8,128)(2,1)S(1)}, f32[400,768]{1,0:T(8,128)S(1)}) custom-call(s16[416,256]{1,0:T(8,128)(2,1)S(1)} %collective-permute-done.2.payload, f32[400,256]{1,0:T(8,128)S(1)} %bitcast.29, f32[1,256]{1,0:T(1,128)S(1)} %bitcast.43, ...), custom_call_target="tpu_custom_call" | custom-call | flops 8000000000 | bytes 65536 | tf_op jit(solution)/shard_map/pallas_call | solution.py:291
  25.4 4.4 %collective-permute-done.1.payload = s16[416,256]{1,0:T(8,128)(2,1)S(1)} collective-permute-done((s16[416,256]{1,0:T(8,128)(2,1)S(1)}, s16[416,256]{1,0:T(8,128)(2,1)S(1)}, u32[]{:S(2)}, u32[]{:S(2)}) %collective-permute-start.1) | collective-permute-done | bytes 213024 | tf_op jit(solution)/shard_map/ppermute | solution.py:304
  29.8 0.7 %shard_map.157 = (bf16[400,768]{1,0:T(8,128)(2,1)S(1)}, bf16[400,768]{1,0:T(8,128)(2,1)S(1)}, s32[8,768]{1,0:T(8,128)S(1)}) custom-call(s16[416,256]{1,0:T(8,128)(2,1)S(1)} %collective-permute-done.1.payload, f32[16,400]{1,0:T(8,128)S(1)} %copy-done), custom_call_target="tpu_custom_call" | custom-call | flops 1000000 | bytes 65536 | tf_op jit(solution)/shard_map/pallas_call | solution.py:291
  30.5 0.0 collective-permute-done.payload
  30.5 5.8 %shard_map.160 = (f32[400,256]{1,0:T(8,128)}, f32[1,256]{1,0:T(1,128)}, f32[400,256]{1,0:T(8,128)S(1)}, f32[1,256]{1,0:T(1,128)S(1)}, bf16[256,768]{1,0:T(8,128)...) custom-call(s16[416,256]{1,0:T(8,128)(2,1)S(1)} %collective-permute-done.payload, ...), custom_call_target="tpu_custom_call" | custom-call | flops 1000000000 | bytes 65536 | tf_op jit(solution)/shard_map/pallas_call | solution.py:291
  36.2 6.5 %all-to-all-start = ((bf16[4,208,128]{2,1,0:T(8,128)(2,1)}), bf16[4,208,128]{2,1,0:T(8,128)(2,1)S(1)}, u32[]{:S(2)}, u32[]{:S(2)}) async-start(bf16[4,208,128]{2,1,0:T(8,128)(2,1)} %get-tuple-element.56), calls=%async_computation | async-start | bytes 425984 | tf_op jit(solution)/shard_map/all_to_all | solution.py:352
  42.7 1.5 %shard_map.161 = (f32[400,256]{1,0:T(8,128)}, f32[1,256]{1,0:T(1,128)}) custom-call(f32[400,256]{1,0:T(8,128)S(1)} %get-tuple-element.50.target, f32[1,256]{1,0:T(1,128)S(1)} %get-tuple-element.51.state, bf16[400,768]{1,0:T(8,128)(2,1)S(1)} %get-tuple-element.43.q_high, bf16[400,768]{1,0:T(8,128)(2,1)S(1)} %get-tuple-element.44.q_low, ...), custom_call_target="tpu_custom_call" | custom-call | flops 1000000000 | bytes 65536 | tf_op jit(solution)/shard_map/pallas_call | solution.py:291
  44.3 4.6 %all-to-all-done.incoming = bf16[4,208,128]{2,1,0:T(8,128)(2,1)S(1)} async-done(((bf16[4,208,128]{2,1,0:T(8,128)(2,1)}), bf16[4,208,128]{2,1,0:T(8,128)(2,1)S(1)}, u32[]{:S(2)}, u32[]{:S(2)}) %all-to-all-start) | async-done | bytes 213024 | tf_op jit(solution)/shard_map/all_to_all | solution.py:352
  48.9 1.3 %shard_map.162 = bf16[4,400,256]{2,1,0:T(8,128)(2,1)} custom-call(bf16[4,208,128]{2,1,0:T(8,128)(2,1)S(1)} %all-to-all-done.incoming), custom_call_target="tpu_custom_call" | custom-call | flops 1000000000 | bytes 65536 | tf_op jit(solution)/shard_map/pallas_call | solution.py:291
Async XLA Ops:
  0.6 1.0 %copy-start.1 = (f32[1,1,256,400]{2,3,1,0:T(8,128)S(1)}, f32[1,1,256,400]{2,3,1,0:T(8,128)}, u32[]{:S(2)}) copy-start(f32[1,1,256,400]{2,3,1,0:T(8,128)} %param.14) | copy-start | bytes 1228804
  1.6 4.3 %copy-start.2 = (f32[1,1,256,400]{2,3,1,0:T(8,128)S(1)}, f32[1,1,256,400]{2,3,1,0:T(8,128)}, u32[]{:S(2)}) copy-start(f32[1,1,256,400]{2,3,1,0:T(8,128)} %param.12) | copy-start | bytes 1228804
  1.6 4.3 %copy-start.3 = (s32[1,1,2,8,128]{4,3,2,1,0:T(8,128)S(1)}, s32[1,1,2,8,128]{4,3,2,1,0:T(8,128)}, u32[]{:S(2)}) copy-start(s32[1,1,2,8,128]{4,3,2,1,0:T(8,128)} %param.17) | copy-start | bytes 24580
  1.6 4.3 %copy-start.4 = (s32[1,1,2,8,128]{4,3,2,1,0:T(8,128)S(1)}, s32[1,1,2,8,128]{4,3,2,1,0:T(8,128)}, u32[]{:S(2)}) copy-start(s32[1,1,2,8,128]{4,3,2,1,0:T(8,128)} %param.18) | copy-start | bytes 24580
  1.6 4.3 %copy-start.5 = (s32[1,1,2,8,128]{4,3,2,1,0:T(8,128)S(1)}, s32[1,1,2,8,128]{4,3,2,1,0:T(8,128)}, u32[]{:S(2)}) copy-start(s32[1,1,2,8,128]{4,3,2,1,0:T(8,128)} %param.19) | copy-start | bytes 24580
  1.6 4.3 %copy-start.6 = (f32[1,1,256]{2,1,0:T(1,128)S(1)}, f32[1,1,256]{2,1,0:T(1,128)}, u32[]{:S(2)}) copy-start(f32[1,1,256]{2,1,0:T(1,128)} %param.15) | copy-start | bytes 3076
  1.7 4.3 %copy-start.7 = (s32[1,1,2,8]{3,2,1,0:T(2,128)S(1)}, s32[1,1,2,8]{3,2,1,0:T(2,128)}, u32[]{:S(2)}) copy-start(s32[1,1,2,8]{3,2,1,0:T(2,128)} %param.20) | copy-start | bytes 196
  1.7 4.3 %copy-start.8 = (s32[1,1,2,8]{3,2,1,0:T(2,128)S(1)}, s32[1,1,2,8]{3,2,1,0:T(2,128)}, u32[]{:S(2)}) copy-start(s32[1,1,2,8]{3,2,1,0:T(2,128)} %param.21) | copy-start | bytes 196
  1.8 20.4 %collective-permute-start.2 = (s16[416,256]{1,0:T(8,128)(2,1)S(1)}, s16[416,256]{1,0:T(8,128)(2,1)S(1)}, u32[]{:S(2)}, u32[]{:S(2)}) collective-permute-start(s16[416,256]{1,0:T(8,128)(2,1)S(1)} %shard_map.155.near), channel_id=1, source_target_pairs={{508,0},{0,4},{4,8},{8,12},{12,16},{16,20},{20,24},{24,28},{28,32}... | collective-permute-start | bytes 638984 | tf_op jit(solution)/shard_map/ppermute | solution.py:304
  6.0 7.4 %copy-start = (f32[16,400]{1,0:T(8,128)S(1)}, f32[16,400]{1,0:T(8,128)}, u32[]{:S(2)}) copy-start(f32[16,400]{1,0:T(8,128)} %relation.5) | copy-start | bytes 76804
  6.0 7.4 %copy-start.9 = (s32[1,1,256]{2,1,0:T(1,128)S(1)}, s32[1,1,256]{2,1,0:T(1,128)}, u32[]{:S(2)}) copy-start(s32[1,1,256]{2,1,0:T(1,128)} %param.22) | copy-start | bytes 3076
  6.0 7.4 %copy-start.10 = (s32[1,1,256]{2,1,0:T(1,128)S(1)}, s32[1,1,256]{2,1,0:T(1,128)}, u32[]{:S(2)}) copy-start(s32[1,1,256]{2,1,0:T(1,128)} %param.23) | copy-start | bytes 3076
  7.0 22.8 %collective-permute-start.1 = (s16[416,256]{1,0:T(8,128)(2,1)S(1)}, s16[416,256]{1,0:T(8,128)(2,1)S(1)}, u32[]{:S(2)}, u32[]{:S(2)}) collective-permute-start(s16[416,256]{1,0:T(8,128)(2,1)S(1)} %get-tuple-element.32), channel_id=1, source_target_pairs={{508,0},{0,4},{4,8},{8,12},{12,16},{16,20},{20,24},{24,28},{28,32}... | collective-permute-start | bytes 638984 | tf_op jit(solution)/shard_map/ppermute | solution.py:304
  10.2 20.3 %collective-permute-start = (s16[416,256]{1,0:T(8,128)(2,1)S(1)}, s16[416,256]{1,0:T(8,128)(2,1)S(1)}, u32[]{:S(2)}, u32[]{:S(2)}) collective-permute-start(s16[416,256]{1,0:T(8,128)(2,1)S(1)} %get-tuple-element.31), channel_id=1, source_target_pairs={{504,0},{508,4},{0,8},{4,12},{8,16},{12,20},{16,24},{20,28},{24,32... | collective-permute-start | bytes 638984 | tf_op jit(solution)/shard_map/ppermute | solution.py:304
  13.4 8.8 %copy-start.11 = (f32[1,1,256]{2,1,0:T(1,128)S(1)}, f32[1,1,256]{2,1,0:T(1,128)}, u32[]{:S(2)}) copy-start(f32[1,1,256]{2,1,0:T(1,128)} %param.13) | copy-start | bytes 3076
  36.2 12.6 %all-to-all-start = ((bf16[4,208,128]{2,1,0:T(8,128)(2,1)}), bf16[4,208,128]{2,1,0:T(8,128)(2,1)S(1)}, u32[]{:S(2)}, u32[]{:S(2)}) async-start(bf16[4,208,128]{2,1,0:T(8,128)(2,1)} %get-tuple-element.56), calls=%async_computation | async-start | bytes 425984 | tf_op jit(solution)/shard_map/all_to_all | solution.py:352

commit v3 on v2

--- a/solution.py
+++ b/solution.py
@@ -259,7 +259,10 @@
     publish(updated, top[...], bottom[...], outgoing)
 
 
-def last_target_kernel(target, state, q_high, q_low, g_high, g_low, new_target, new_state):
+def last_target_kernel(target, state, q_high, q_low, g_high, g_low, source, source_state,
+                       new_target, new_state, new_source, new_source_state):
+    new_source[...] = source[...]
+    new_source_state[...] = source_state[...]
     gradient = jnp.zeros(target.shape, F32)
     for first in range(0, LIVE, CHUNK):
         at = pl.ds(first, CHUNK)
@@ -267,20 +270,24 @@
     new_target[...], new_state[...] = adagrad(target[...], state[...], gradient)
 
 
-def serve_kernel(incoming, served):
+def serve_kernel(incoming, served, spread, sems):
     shards, packed_rows, lanes = incoming.shape
-    half = served.shape[1] // 2
-    rows = served.shape[2]
+    half = spread.shape[1] // 2
+    rows = spread.shape[2]
     lane = lax.broadcasted_iota(jnp.int32, (rows, lanes), 1)
     number = (lax.broadcasted_iota(jnp.int32, (rows, lanes), 0) + 1).astype(F32)
+    copies = []
     for s in range(shards):
         block = incoming[s]
-        index = block[half : half + 8].astype(F32)[:1]
-        match = number == index
+        match = number == block[half : half + 8].astype(F32)[:1]
         top = jnp.logical_and(match, lane < SLOTS).astype(F32)
         bottom = jnp.logical_and(match, lane >= SLOTS).astype(F32)
-        spread = dot(block, jnp.concatenate([top, bottom], axis=0).astype(BF16), NT)
-        served[s] = jnp.concatenate([spread[:half, :rows], spread[:half, rows:]], axis=0).astype(BF16)
+        both = dot(block, jnp.concatenate([top, bottom], axis=0).astype(BF16), NT)
+        spread[s] = jnp.concatenate([both[:half, :rows], both[:half, rows:]], axis=0).astype(BF16)
+        copies.append(pltpu.make_async_copy(spread.at[s], served.at[s], sems.at[s]))
+        copies[-1].start()
+    for copy in copies:
+        copy.wait()
 
 
 VMEM = pl.BlockSpec(memory_space=pltpu.VMEM)
@@ -350,8 +357,17 @@
         main_kernel, [matrix, line, matrix, line, grad16, grad16, ((shards, width // 2 + 8, 2 * SLOTS), BF16)],
         (far_target, behind_high, behind_low, behind_ids, source, source_sums, ids_next, q_high, q_low, relation, top, bottom))
     incoming = lax.all_to_all(outgoing, "serve", split_axis=0, concat_axis=0, tiled=True)
-    target, target_sums = call(last_target_kernel, [matrix, line], (target, target_sums, q_high, q_low, g_high, g_low))
-    served = call(serve_kernel, [((shards, width, rows), BF16)], (incoming,))[0]
+    target, target_sums, source, source_sums = call(
+        last_target_kernel, [matrix, line, matrix, line],
+        (target, target_sums, q_high, q_low, g_high, g_low, source, source_sums))
+    served = pl.pallas_call(
+        serve_kernel,
+        out_shape=jax.ShapeDtypeStruct((shards, width, rows), BF16),
+        in_specs=[VMEM],
+        out_specs=pl.BlockSpec(memory_space=pl.ANY),
+        scratch_shapes=[pltpu.VMEM((shards, width, rows), BF16), pltpu.SemaphoreType.DMA((shards,))],
+        compiler_params=pltpu.CompilerParams(vmem_limit_bytes=40 * 2**20),
+    )(incoming)
     return (
         jnp.swapaxes(source, 0, 1)[None, None],
         source_sums[None],

time: 50.5 us -> 50.3 us (level)
    pallas_call x8 -> x7, Pallas kernels: 15.3 us -> 14 us  [call(): pl.pallas_call(kernel, out_shape=[jax.ShapeDtypeStruct(shape, kind) for s...]
    pallas_call x0 -> x1, Pallas kernels: none -> 1.14 us  [on_device(): pl.pallas_call(serve_kernel, out_shape=jax.ShapeDtypeStruct((shards, widt...]
where the time goes in v3:
time: 50.3 us; the launch traced here: 50 us
  starting transfers between devices  16.9 us (34%)
  waiting for transfers between devices  16 us (32%)
  Pallas kernels  15.2 us (30%)
  local copies, waits for them, and re-layouts  1.05 us (2%)
  between operations  0.85 us (2%)
    pallas_call x7, Pallas kernels, call(): pl.pallas_call(kernel, out_shape=[jax.ShapeDtypeStruct(shape, kind) for s...  14 us
    ppermute x3, waiting for transfers between devices, from_behind(): return lax.ppermute(block, axis, route)  11.5 us
    ppermute x3, starting transfers between devices, from_behind(): return lax.ppermute(block, axis, route)  10.5 us
    all_to_all x1, starting transfers between devices, on_device(): lax.all_to_all(outgoing, 'serve', split_axis=0, concat_axis=0, tiled=True)  6.48 us
    all_to_all x1, waiting for transfers between devices, on_device(): lax.all_to_all(outgoing, 'serve', split_axis=0, concat_axis=0, tiled=True)  4.53 us
    pallas_call x1, Pallas kernels, on_device(): pl.pallas_call(serve_kernel, out_shape=jax.ShapeDtypeStruct((shards, widt...  1.14 us
    unnamed x24, local copies, waits for them, and re-layouts  1.05 us
  transfers between devices with their start and end apart: 4, of which 3 were waited for; matrix products, arithmetic and copies ran while one was open for 0% of the time, Pallas kernels for 16%

profile of v3, /device:TPU:1, one launch (start us, length us, event | category | flops | bytes accessed | tf_op | source)
XLA Modules:
  0.0 50.0 jit_solution(1734221705852162389)
XLA Ops:
  0.6 0.0 copy-start.1
  0.6 1.0 %copy-done.1 = f32[1,1,256,400]{2,3,1,0:T(8,128)S(1)} copy-done((f32[1,1,256,400]{2,3,1,0:T(8,128)S(1)}, f32[1,1,256,400]{2,3,1,0:T(8,128)}, u32[]{:S(2)}) %copy-start.1) | copy-done | bytes 409624
  1.6 0.0 copy-start.2
  1.6 0.0 copy-start.3
  1.6 0.0 copy-start.4
  1.6 0.0 copy-start.5
  1.6 0.0 copy-start.6
  1.7 0.0 copy-start.7
  1.7 0.0 copy-start.8
  1.7 0.1 shard_map.155.near
  1.8 4.1 %collective-permute-start.2 = (s16[416,256]{1,0:T(8,128)(2,1)S(1)}, s16[416,256]{1,0:T(8,128)(2,1)S(1)}, u32[]{:S(2)}, u32[]{:S(2)}) collective-permute-start(s16[416,256]{1,0:T(8,128)(2,1)S(1)} %shard_map.155.near), channel_id=1, source_target_pairs={{508,0},{0,4},{4,8},{8,12},{12,16},{16,20},{20,24},{24,28},{28,32}... | collective-permute-start | bytes 638984 | tf_op jit(solution)/shard_map/ppermute | solution.py:311
  5.9 0.0 copy-done.2
  5.9 0.0 copy-done.3
  5.9 0.0 copy-done.4
  5.9 0.0 copy-done.5
  5.9 0.0 copy-done.6
  6.0 0.0 copy-done.7
  6.0 0.0 copy-done.8
  6.0 0.0 copy-start
  6.0 0.0 copy-start.9
  6.0 0.0 copy-start.10
  6.0 1.0 %shard_map.156 = (s16[416,256]{1,0:T(8,128)(2,1)S(1)}, s16[416,256]{1,0:T(8,128)(2,1)S(1)}, s32[8,768]{1,0:T(8,128)S(1)}) custom-call(f32[400,256]{1,0:T(8,128)S(1)} %bitcast.27, s32[2,8,128]{2,1,0:T(8,128)S(1)} %bitcast.30, s32[2,8,128]{2,1,0:T(8,128)S(1)} %bitcast.32, s32[2,8,128]{2,1,0:T(8,128)S(1)} %bitcast.34, s32[2,8]{1,0:T(2,128)S(1)} %bitcast.37, ...), custom_call_target="tpu_custom_call" | custom-call | flops 1000000000 | bytes 65536 | tf_op jit(solution)/shard_map/pallas_call | solution.py:298
  7.0 3.2 %collective-permute-start.1 = (s16[416,256]{1,0:T(8,128)(2,1)S(1)}, s16[416,256]{1,0:T(8,128)(2,1)S(1)}, u32[]{:S(2)}, u32[]{:S(2)}) collective-permute-start(s16[416,256]{1,0:T(8,128)(2,1)S(1)} %get-tuple-element.34), channel_id=1, source_target_pairs={{508,0},{0,4},{4,8},{8,12},{12,16},{16,20},{20,24},{24,28},{28,32}... | collective-permute-start | bytes 638984 | tf_op jit(solution)/shard_map/ppermute | solution.py:311
  10.2 3.2 %collective-permute-start = (s16[416,256]{1,0:T(8,128)(2,1)S(1)}, s16[416,256]{1,0:T(8,128)(2,1)S(1)}, u32[]{:S(2)}, u32[]{:S(2)}) collective-permute-start(s16[416,256]{1,0:T(8,128)(2,1)S(1)} %get-tuple-element.33), channel_id=1, source_target_pairs={{504,0},{508,4},{0,8},{4,12},{8,16},{12,20},{16,24},{20,28},{24,32... | collective-permute-start | bytes 638984 | tf_op jit(solution)/shard_map/ppermute | solution.py:311
  13.4 0.0 copy-done
  13.4 0.0 copy-done.9
  13.4 0.0 copy-done.10
  13.4 0.0 copy-start.11
  13.4 1.7 %shard_map.158 = (bf16[400,768]{1,0:T(8,128)(2,1)S(1)}, bf16[400,768]{1,0:T(8,128)(2,1)S(1)}, f32[400,768]{1,0:T(8,128)S(1)}, s32[8,768]{1,0:T(8,128)S(1)}, bf16...) custom-call(f32[400,256]{1,0:T(8,128)S(1)} %bitcast.28, f32[16,400]{1,0:T(8,128)S(1)} %copy-done, ...), custom_call_target="tpu_custom_call" | custom-call | flops 1000000000 | bytes 65536 | tf_op jit(solution)/shard_map/pallas_call | solution.py:298
  15.2 7.1 %collective-permute-done.2.payload = s16[416,256]{1,0:T(8,128)(2,1)S(1)} collective-permute-done((s16[416,256]{1,0:T(8,128)(2,1)S(1)}, s16[416,256]{1,0:T(8,128)(2,1)S(1)}, u32[]{:S(2)}, u32[]{:S(2)}) %collective-permute-start.2) | collective-permute-done | bytes 213024 | tf_op jit(solution)/shard_map/ppermute | solution.py:311
  22.2 0.0 copy-done.11
  22.2 3.1 %shard_map.159 = (f32[400,256]{1,0:T(8,128)S(1)}, f32[1,256]{1,0:T(1,128)S(1)}, bf16[400,768]{1,0:T(8,128)(2,1)S(1)}, bf16[400,768]{1,0:T(8,128)(2,1)S(1)}, f32[400,768]{1,0:T(8,128)S(1)}) custom-call(s16[416,256]{1,0:T(8,128)(2,1)S(1)} %collective-permute-done.2.payload, f32[400,256]{1,0:T(8,128)S(1)} %bitcast.29, f32[1,256]{1,0:T(1,128)S(1)} %bitcast.43, ...), custom_call_target="tpu_custom_call" | custom-call | flops 8000000000 | bytes 65536 | tf_op jit(solution)/shard_map/pallas_call | solution.py:298
  25.4 4.4 %collective-permute-done.1.payload = s16[416,256]{1,0:T(8,128)(2,1)S(1)} collective-permute-done((s16[416,256]{1,0:T(8,128)(2,1)S(1)}, s16[416,256]{1,0:T(8,128)(2,1)S(1)}, u32[]{:S(2)}, u32[]{:S(2)}) %collective-permute-start.1) | collective-permute-done | bytes 213024 | tf_op jit(solution)/shard_map/ppermute | solution.py:311
  29.8 0.7 %shard_map.157 = (bf16[400,768]{1,0:T(8,128)(2,1)S(1)}, bf16[400,768]{1,0:T(8,128)(2,1)S(1)}, s32[8,768]{1,0:T(8,128)S(1)}) custom-call(s16[416,256]{1,0:T(8,128)(2,1)S(1)} %collective-permute-done.1.payload, f32[16,400]{1,0:T(8,128)S(1)} %copy-done), custom_call_target="tpu_custom_call" | custom-call | flops 1000000 | bytes 65536 | tf_op jit(solution)/shard_map/pallas_call | solution.py:298
  30.5 0.0 collective-permute-done.payload
  30.5 5.7 %shard_map.160 = (f32[400,256]{1,0:T(8,128)S(1)}, f32[1,256]{1,0:T(1,128)S(1)}, f32[400,256]{1,0:T(8,128)S(1)}, f32[1,256]{1,0:T(1,128)S(1)}, bf16[256,768]{1,0:...) custom-call(s16[416,256]{1,0:T(8,128)(2,1)S(1)} %collective-permute-done.payload, ...), custom_call_target="tpu_custom_call" | custom-call | flops 1000000000 | bytes 65536 | tf_op jit(solution)/shard_map/pallas_call | solution.py:298
  36.2 6.5 %all-to-all-start = ((bf16[4,208,128]{2,1,0:T(8,128)(2,1)}), bf16[4,208,128]{2,1,0:T(8,128)(2,1)S(1)}, u32[]{:S(2)}, u32[]{:S(2)}) async-start(bf16[4,208,128]{2,1,0:T(8,128)(2,1)} %get-tuple-element.60), calls=%async_computation | async-start | bytes 425984 | tf_op jit(solution)/shard_map/all_to_all | solution.py:359
  42.7 1.6 %shard_map.161 = (f32[400,256]{1,0:T(8,128)}, f32[1,256]{1,0:T(1,128)}, f32[400,256]{1,0:T(8,128)}, f32[1,256]{1,0:T(1,128)}) custom-call(f32[400,256]{1,0:T(8,128)S(1)} %get-tuple-element.50.target, f32[1,256]{1,0:T(1,128)S(1)} %get-tuple-element.51.state, bf16[400,768]{1,0:T(8,128)(2,1)S(1)} %get-tuple-element.45.q_high, ...), custom_call_target="tpu_custom_call" | custom-call | flops 1000000000 | bytes 65536 | tf_op jit(solution)/shard_map/pallas_call | solution.py:298
  44.3 4.5 %all-to-all-done.incoming = bf16[4,208,128]{2,1,0:T(8,128)(2,1)S(1)} async-done(((bf16[4,208,128]{2,1,0:T(8,128)(2,1)}), bf16[4,208,128]{2,1,0:T(8,128)(2,1)S(1)}, u32[]{:S(2)}, u32[]{:S(2)}) %all-to-all-start) | async-done | bytes 213024 | tf_op jit(solution)/shard_map/all_to_all | solution.py:359
  48.9 1.1 %shard_map.162 = bf16[4,400,256]{2,1,0:T(8,128)(2,1)} custom-call(bf16[4,208,128]{2,1,0:T(8,128)(2,1)S(1)} %all-to-all-done.incoming), custom_call_target="tpu_custom_call" | custom-call | tf_op jit(solution)/shard_map/pallas_call | solution.py:363
Async XLA Ops:
  0.6 1.0 %copy-start.1 = (f32[1,1,256,400]{2,3,1,0:T(8,128)S(1)}, f32[1,1,256,400]{2,3,1,0:T(8,128)}, u32[]{:S(2)}) copy-start(f32[1,1,256,400]{2,3,1,0:T(8,128)} %param.14) | copy-start | bytes 1228804
  1.6 4.3 %copy-start.2 = (f32[1,1,256,400]{2,3,1,0:T(8,128)S(1)}, f32[1,1,256,400]{2,3,1,0:T(8,128)}, u32[]{:S(2)}) copy-start(f32[1,1,256,400]{2,3,1,0:T(8,128)} %param.12) | copy-start | bytes 1228804
  1.6 4.3 %copy-start.3 = (s32[1,1,2,8,128]{4,3,2,1,0:T(8,128)S(1)}, s32[1,1,2,8,128]{4,3,2,1,0:T(8,128)}, u32[]{:S(2)}) copy-start(s32[1,1,2,8,128]{4,3,2,1,0:T(8,128)} %param.17) | copy-start | bytes 24580
  1.6 4.3 %copy-start.4 = (s32[1,1,2,8,128]{4,3,2,1,0:T(8,128)S(1)}, s32[1,1,2,8,128]{4,3,2,1,0:T(8,128)}, u32[]{:S(2)}) copy-start(s32[1,1,2,8,128]{4,3,2,1,0:T(8,128)} %param.18) | copy-start | bytes 24580
  1.6 4.3 %copy-start.5 = (s32[1,1,2,8,128]{4,3,2,1,0:T(8,128)S(1)}, s32[1,1,2,8,128]{4,3,2,1,0:T(8,128)}, u32[]{:S(2)}) copy-start(s32[1,1,2,8,128]{4,3,2,1,0:T(8,128)} %param.19) | copy-start | bytes 24580
  1.6 4.3 %copy-start.6 = (f32[1,1,256]{2,1,0:T(1,128)S(1)}, f32[1,1,256]{2,1,0:T(1,128)}, u32[]{:S(2)}) copy-start(f32[1,1,256]{2,1,0:T(1,128)} %param.15) | copy-start | bytes 3076
  1.7 4.3 %copy-start.7 = (s32[1,1,2,8]{3,2,1,0:T(2,128)S(1)}, s32[1,1,2,8]{3,2,1,0:T(2,128)}, u32[]{:S(2)}) copy-start(s32[1,1,2,8]{3,2,1,0:T(2,128)} %param.20) | copy-start | bytes 196
  1.7 4.3 %copy-start.8 = (s32[1,1,2,8]{3,2,1,0:T(2,128)S(1)}, s32[1,1,2,8]{3,2,1,0:T(2,128)}, u32[]{:S(2)}) copy-start(s32[1,1,2,8]{3,2,1,0:T(2,128)} %param.21) | copy-start | bytes 196
  1.8 20.4 %collective-permute-start.2 = (s16[416,256]{1,0:T(8,128)(2,1)S(1)}, s16[416,256]{1,0:T(8,128)(2,1)S(1)}, u32[]{:S(2)}, u32[]{:S(2)}) collective-permute-start(s16[416,256]{1,0:T(8,128)(2,1)S(1)} %shard_map.155.near), channel_id=1, source_target_pairs={{508,0},{0,4},{4,8},{8,12},{12,16},{16,20},{20,24},{24,28},{28,32}... | collective-permute-start | bytes 638984 | tf_op jit(solution)/shard_map/ppermute | solution.py:311
  6.0 7.4 %copy-start = (f32[16,400]{1,0:T(8,128)S(1)}, f32[16,400]{1,0:T(8,128)}, u32[]{:S(2)}) copy-start(f32[16,400]{1,0:T(8,128)} %relation.5) | copy-start | bytes 76804
  6.0 7.4 %copy-start.9 = (s32[1,1,256]{2,1,0:T(1,128)S(1)}, s32[1,1,256]{2,1,0:T(1,128)}, u32[]{:S(2)}) copy-start(s32[1,1,256]{2,1,0:T(1,128)} %param.22) | copy-start | bytes 3076
  6.0 7.4 %copy-start.10 = (s32[1,1,256]{2,1,0:T(1,128)S(1)}, s32[1,1,256]{2,1,0:T(1,128)}, u32[]{:S(2)}) copy-start(s32[1,1,256]{2,1,0:T(1,128)} %param.23) | copy-start | bytes 3076
  7.0 22.8 %collective-permute-start.1 = (s16[416,256]{1,0:T(8,128)(2,1)S(1)}, s16[416,256]{1,0:T(8,128)(2,1)S(1)}, u32[]{:S(2)}, u32[]{:S(2)}) collective-permute-start(s16[416,256]{1,0:T(8,128)(2,1)S(1)} %get-tuple-element.34), channel_id=1, source_target_pairs={{508,0},{0,4},{4,8},{8,12},{12,16},{16,20},{20,24},{24,28},{28,32}... | collective-permute-start | bytes 638984 | tf_op jit(solution)/shard_map/ppermute | solution.py:311
  10.2 20.3 %collective-permute-start = (s16[416,256]{1,0:T(8,128)(2,1)S(1)}, s16[416,256]{1,0:T(8,128)(2,1)S(1)}, u32[]{:S(2)}, u32[]{:S(2)}) collective-permute-start(s16[416,256]{1,0:T(8,128)(2,1)S(1)} %get-tuple-element.33), channel_id=1, source_target_pairs={{504,0},{508,4},{0,8},{4,12},{8,16},{12,20},{16,24},{20,28},{24,32... | collective-permute-start | bytes 638984 | tf_op jit(solution)/shard_map/ppermute | solution.py:311
  13.4 8.8 %copy-start.11 = (f32[1,1,256]{2,1,0:T(1,128)S(1)}, f32[1,1,256]{2,1,0:T(1,128)}, u32[]{:S(2)}) copy-start(f32[1,1,256]{2,1,0:T(1,128)} %param.13) | copy-start | bytes 3076
  36.2 12.6 %all-to-all-start = ((bf16[4,208,128]{2,1,0:T(8,128)(2,1)}), bf16[4,208,128]{2,1,0:T(8,128)(2,1)S(1)}, u32[]{:S(2)}, u32[]{:S(2)}) async-start(bf16[4,208,128]{2,1,0:T(8,128)(2,1)} %get-tuple-element.60), calls=%async_computation | async-start | bytes 425984 | tf_op jit(solution)/shard_map/all_to_all | solution.py:359

commit v4 on v3

--- a/solution.py
+++ b/solution.py
@@ -226,21 +226,26 @@
         outgoing[s] = packed[:, s * 2 * SLOTS : (s + 1) * 2 * SLOTS]
 
 
-def main_kernel(payload, behind_high, behind_low, behind_ids, source, state, ids, q_high, q_low, rel_in, top, bottom,
+def far_kernel(payload, target, state, parts):
+    width = target.shape[0]
+    packed = payload[...].astype(jnp.int32)
+    rows = decoded(packed[:width], packed[width : width + 1])
+    tail = packed[width:].astype(F32)
+    state[...] = (tail[1:2] + tail[2:3] * (1.0 / SCALE_UNIT)) * (1.0 / SCALE_UNIT)
+    target[...] = rows
+    parts[...] = row_major(*halves(rows))
+
+
+def main_kernel(far_target, far_state, far_parts, behind_high, behind_low, behind_ids, source, state, ids, q_high, q_low, rel_in, top, bottom,
                 new_source, new_state, new_target, new_target_state, g_high, g_low, outgoing):
-    width, rows = source.shape
-    packed = payload[...].astype(jnp.int32)
-    target = decoded(packed[:width], packed[width : width + 1])
-    tail = packed[width:].astype(F32)
-    target_state = (tail[1:2] + tail[2:3] * (1.0 / SCALE_UNIT)) * (1.0 / SCALE_UNIT)
-    parts = row_major(*halves(target))
+    parts = far_parts[...]
     gradient = jnp.zeros(source.shape, F32)
     for first in range(0, LIVE, CHUNK):
         at = pl.ds(first, CHUNK)
         qh, ql = behind_high[:, at], behind_low[:, at]
         gh, gl = score_gradients(parts, qh, ql, behind_ids[1:2, at], behind_ids[3:4, at])
         gradient += target_gradient(qh, ql, gh, gl)
-    target, sums = adagrad(target, target_state, gradient)
+    target, sums = adagrad(far_target[...], far_state[...], gradient)
     new_target[...] = target
     new_target_state[...] = sums
     high, low = halves(target)
@@ -351,11 +356,15 @@
     source, source_sums, q_high, q_low, relation = call(
         source_kernel, [matrix, line, edge16, edge16, edge32],
         (near_target, source, source_sums, relation_table, ids, ids_next, q_high, q_low, relation), flops=8 * 10**9)
+    far_target = lax.optimization_barrier((far_target, source_sums))[0]
+    far_rows, far_state, far_parts = call(
+        far_kernel, [matrix, line, ((rows, 3 * width), BF16)], (far_target,), flops=10**6)
+    near_source = lax.optimization_barrier((near_source, far_state))[0]
     behind_high, behind_low, behind_ids = call(
         behind_kernel, [edge16, edge16, ids8], (near_source, relation_table), flops=10**6)
     source, source_sums, target, target_sums, g_high, g_low, outgoing = call(
         main_kernel, [matrix, line, matrix, line, grad16, grad16, ((shards, width // 2 + 8, 2 * SLOTS), BF16)],
-        (far_target, behind_high, behind_low, behind_ids, source, source_sums, ids_next, q_high, q_low, relation, top, bottom))
+        (far_rows, far_state, far_parts, behind_high, behind_low, behind_ids, source, source_sums, ids_next, q_high, q_low, relation, top, bottom))
     incoming = lax.all_to_all(outgoing, "serve", split_axis=0, concat_axis=0, tiled=True)
     target, target_sums, source, source_sums = call(
         last_target_kernel, [matrix, line, matrix, line],

time: 50.3 us -> 50.4 us (level)
  starting transfers between devices: 16.9 us -> 15.7 us
  waiting for transfers between devices: 16 us -> 17.2 us
    all_to_all x1, starting transfers between devices: 6.48 us -> 5.23 us  [on_device(): lax.all_to_all(outgoing, 'serve', split_axis=0, concat_axis=0, tiled=True)]
    ppermute x3, waiting for transfers between devices: 11.5 us -> 12.7 us  [from_behind(): return lax.ppermute(block, axis, route)]
    pallas_call x7 -> x8, Pallas kernels: 14 us -> 14.1 us  [call(): pl.pallas_call(kernel, out_shape=[jax.ShapeDtypeStruct(shape, kind) for s...]
  transfers between devices with their start and end apart: 4 -> 4, of which waited for: 3 -> 4; matrix products, arithmetic and copies ran while one was open for 0% -> 0% of each run, Pallas kernels for 16% -> 16%
where the time goes in v4:
time: 50.4 us; the launch traced here: 50.1 us
  waiting for transfers between devices  17.2 us (34%)
  starting transfers between devices  15.7 us (31%)
  Pallas kernels  15.3 us (30%)
  local copies, waits for them, and re-layouts  1.05 us (2%)
  between operations  0.85 us (2%)
    pallas_call x8, Pallas kernels, call(): pl.pallas_call(kernel, out_shape=[jax.ShapeDtypeStruct(shape, kind) for s...  14.1 us
    ppermute x3, waiting for transfers between devices, from_behind(): return lax.ppermute(block, axis, route)  12.7 us
    ppermute x3, starting transfers between devices, from_behind(): return lax.ppermute(block, axis, route)  10.5 us
    all_to_all x1, starting transfers between devices, on_device(): lax.all_to_all(outgoing, 'serve', split_axis=0, concat_axis=0, tiled=True)  5.23 us
    all_to_all x1, waiting for transfers between devices, on_device(): lax.all_to_all(outgoing, 'serve', split_axis=0, concat_axis=0, tiled=True)  4.53 us
    pallas_call x1, Pallas kernels, on_device(): pl.pallas_call(serve_kernel, out_shape=jax.ShapeDtypeStruct((shards, widt...  1.14 us
    unnamed x24, local copies, waits for them, and re-layouts  1.05 us
  transfers between devices with their start and end apart: 4, of which 4 were waited for; matrix products, arithmetic and copies ran while one was open for 0% of the time, Pallas kernels for 16%

profile of v4, /device:TPU:1, one launch (start us, length us, event | category | flops | bytes accessed | tf_op | source)
XLA Modules:
  0.0 50.1 jit_solution(3040960518118174684)
XLA Ops:
  0.6 0.0 copy-start.1
  0.6 1.0 %copy-done.1 = f32[1,1,256,400]{2,3,1,0:T(8,128)S(1)} copy-done((f32[1,1,256,400]{2,3,1,0:T(8,128)S(1)}, f32[1,1,256,400]{2,3,1,0:T(8,128)}, u32[]{:S(2)}) %copy-start.1) | copy-done | bytes 409624
  1.6 0.0 copy-start.2
  1.6 0.0 copy-start.3
  1.6 0.0 copy-start.4
  1.6 0.0 copy-start.5
  1.6 0.0 copy-start.6
  1.7 0.0 copy-start.7
  1.7 0.0 copy-start.8
  1.7 0.1 shard_map.155.near
  1.8 4.1 %collective-permute-start.1 = (s16[416,256]{1,0:T(8,128)(2,1)S(1)}, s16[416,256]{1,0:T(8,128)(2,1)S(1)}, u32[]{:S(2)}, u32[]{:S(2)}) collective-permute-start(s16[416,256]{1,0:T(8,128)(2,1)S(1)} %shard_map.155.near), channel_id=1, source_target_pairs={{508,0},{0,4},{4,8},{8,12},{12,16},{16,20},{20,24},{24,28},{28,32}... | collective-permute-start | bytes 638984 | tf_op jit(solution)/shard_map/ppermute | solution.py:316
  5.9 0.0 copy-done.2
  5.9 0.0 copy-done.3
  5.9 0.0 copy-done.4
  5.9 0.0 copy-done.5
  5.9 0.0 copy-done.6
  6.0 0.0 copy-done.7
  6.0 0.0 copy-done.8
  6.0 0.0 copy-start
  6.0 0.0 copy-start.9
  6.0 0.0 copy-start.10
  6.0 1.0 %shard_map.156 = (s16[416,256]{1,0:T(8,128)(2,1)S(1)}, s16[416,256]{1,0:T(8,128)(2,1)S(1)}, s32[8,768]{1,0:T(8,128)S(1)}) custom-call(f32[400,256]{1,0:T(8,128)S(1)} %bitcast.27, s32[2,8,128]{2,1,0:T(8,128)S(1)} %bitcast.30, s32[2,8,128]{2,1,0:T(8,128)S(1)} %bitcast.32, s32[2,8,128]{2,1,0:T(8,128)S(1)} %bitcast.34, s32[2,8]{1,0:T(2,128)S(1)} %bitcast.37, ...), custom_call_target="tpu_custom_call" | custom-call | flops 1000000000 | bytes 65536 | tf_op jit(solution)/shard_map/pallas_call | solution.py:303
  7.0 3.2 %collective-permute-start = (s16[416,256]{1,0:T(8,128)(2,1)S(1)}, s16[416,256]{1,0:T(8,128)(2,1)S(1)}, u32[]{:S(2)}, u32[]{:S(2)}) collective-permute-start(s16[416,256]{1,0:T(8,128)(2,1)S(1)} %get-tuple-element.38), channel_id=1, source_target_pairs={{504,0},{508,4},{0,8},{4,12},{8,16},{12,20},{16,24},{20,28},{24,32... | collective-permute-start | bytes 638984 | tf_op jit(solution)/shard_map/ppermute | solution.py:316
  10.2 3.2 %collective-permute-start.2 = (s16[416,256]{1,0:T(8,128)(2,1)S(1)}, s16[416,256]{1,0:T(8,128)(2,1)S(1)}, u32[]{:S(2)}, u32[]{:S(2)}) collective-permute-start(s16[416,256]{1,0:T(8,128)(2,1)S(1)} %get-tuple-element.49), channel_id=1, source_target_pairs={{508,0},{0,4},{4,8},{8,12},{12,16},{16,20},{20,24},{24,28},{28,32}... | collective-permute-start | bytes 638984 | tf_op jit(solution)/shard_map/ppermute | solution.py:316
  13.4 0.0 copy-done
  13.4 0.0 copy-done.9
  13.4 0.0 copy-done.10
  13.4 0.0 copy-start.11
  13.4 1.7 %shard_map.157 = (bf16[400,768]{1,0:T(8,128)(2,1)S(1)}, bf16[400,768]{1,0:T(8,128)(2,1)S(1)}, f32[400,768]{1,0:T(8,128)S(1)}, s32[8,768]{1,0:T(8,128)S(1)}, bf16...) custom-call(f32[400,256]{1,0:T(8,128)S(1)} %bitcast.28, f32[16,400]{1,0:T(8,128)S(1)} %copy-done, ...), custom_call_target="tpu_custom_call" | custom-call | flops 1000000000 | bytes 65536 | tf_op jit(solution)/shard_map/pallas_call | solution.py:303
  15.2 7.2 %collective-permute-done.1.payload = s16[416,256]{1,0:T(8,128)(2,1)S(1)} collective-permute-done((s16[416,256]{1,0:T(8,128)(2,1)S(1)}, s16[416,256]{1,0:T(8,128)(2,1)S(1)}, u32[]{:S(2)}, u32[]{:S(2)}) %collective-permute-start.1) | collective-permute-done | bytes 213024 | tf_op jit(solution)/shard_map/ppermute | solution.py:316
  22.4 0.0 copy-done.11
  22.4 3.1 %shard_map.158 = (f32[400,256]{1,0:T(8,128)S(1)}, f32[1,256]{1,0:T(1,128)S(1)}, bf16[400,768]{1,0:T(8,128)(2,1)S(1)}, bf16[400,768]{1,0:T(8,128)(2,1)S(1)}, f32[400,768]{1,0:T(8,128)S(1)}) custom-call(s16[416,256]{1,0:T(8,128)(2,1)S(1)} %collective-permute-done.1.payload, f32[400,256]{1,0:T(8,128)S(1)} %bitcast.29, f32[1,256]{1,0:T(1,128)S(1)} %bitcast.43, ...), custom_call_target="tpu_custom_call" | custom-call | flops 8000000000 | bytes 65536 | tf_op jit(solution)/shard_map/pallas_call | solution.py:303
  25.5 0.7 %collective-permute-done.payload = s16[416,256]{1,0:T(8,128)(2,1)S(1)} collective-permute-done((s16[416,256]{1,0:T(8,128)(2,1)S(1)}, s16[416,256]{1,0:T(8,128)(2,1)S(1)}, u32[]{:S(2)}, u32[]{:S(2)}) %collective-permute-start) | collective-permute-done | bytes 213024 | tf_op jit(solution)/shard_map/ppermute | solution.py:316
  26.2 0.4 shard_map.159
  26.6 4.8 %collective-permute-done.2.payload = s16[416,256]{1,0:T(8,128)(2,1)S(1)} collective-permute-done((s16[416,256]{1,0:T(8,128)(2,1)S(1)}, s16[416,256]{1,0:T(8,128)(2,1)S(1)}, u32[]{:S(2)}, u32[]{:S(2)}) %collective-permute-start.2) | collective-permute-done | bytes 213024 | tf_op jit(solution)/shard_map/ppermute | solution.py:316
  31.4 0.7 %shard_map.160 = (bf16[400,768]{1,0:T(8,128)(2,1)S(1)}, bf16[400,768]{1,0:T(8,128)(2,1)S(1)}, s32[8,768]{1,0:T(8,128)S(1)}) custom-call(s16[416,256]{1,0:T(8,128)(2,1)S(1)} %collective-permute-done.2.payload, f32[16,400]{1,0:T(8,128)S(1)} %copy-done), custom_call_target="tpu_custom_call" | custom-call | flops 1000000 | bytes 65536 | tf_op jit(solution)/shard_map/pallas_call | solution.py:303
  32.1 5.5 %shard_map.161 = (f32[400,256]{1,0:T(8,128)S(1)}, f32[1,256]{1,0:T(1,128)S(1)}, f32[400,256]{1,0:T(8,128)S(1)}, f32[1,256]{1,0:T(1,128)S(1)}, bf16[256,768]{1,0:...) custom-call(f32[400,256]{1,0:T(8,128)S(1)} %get-tuple-element.46.far_target, ...), custom_call_target="tpu_custom_call" | custom-call | flops 1000000000 | bytes 65536 | tf_op jit(solution)/shard_map/pallas_call | solution.py:303
  37.5 5.2 %all-to-all-start = ((bf16[4,208,128]{2,1,0:T(8,128)(2,1)}), bf16[4,208,128]{2,1,0:T(8,128)(2,1)S(1)}, u32[]{:S(2)}, u32[]{:S(2)}) async-start(bf16[4,208,128]{2,1,0:T(8,128)(2,1)} %get-tuple-element.70), calls=%async_computation | async-start | bytes 425984 | tf_op jit(solution)/shard_map/all_to_all | solution.py:368
  42.8 1.6 %shard_map.162 = (f32[400,256]{1,0:T(8,128)}, f32[1,256]{1,0:T(1,128)}, f32[400,256]{1,0:T(8,128)}, f32[1,256]{1,0:T(1,128)}) custom-call(f32[400,256]{1,0:T(8,128)S(1)} %get-tuple-element.60.target, f32[1,256]{1,0:T(1,128)S(1)} %get-tuple-element.61.state, bf16[400,768]{1,0:T(8,128)(2,1)S(1)} %get-tuple-element.55.q_high, ...), custom_call_target="tpu_custom_call" | custom-call | flops 1000000000 | bytes 65536 | tf_op jit(solution)/shard_map/pallas_call | solution.py:303
  44.4 4.5 %all-to-all-done.incoming = bf16[4,208,128]{2,1,0:T(8,128)(2,1)S(1)} async-done(((bf16[4,208,128]{2,1,0:T(8,128)(2,1)}), bf16[4,208,128]{2,1,0:T(8,128)(2,1)S(1)}, u32[]{:S(2)}, u32[]{:S(2)}) %all-to-all-start) | async-done | bytes 213024 | tf_op jit(solution)/shard_map/all_to_all | solution.py:368
  48.9 1.1 %shard_map.163 = bf16[4,400,256]{2,1,0:T(8,128)(2,1)} custom-call(bf16[4,208,128]{2,1,0:T(8,128)(2,1)S(1)} %all-to-all-done.incoming), custom_call_target="tpu_custom_call" | custom-call | tf_op jit(solution)/shard_map/pallas_call | solution.py:372
Async XLA Ops:
  0.6 1.0 %copy-start.1 = (f32[1,1,256,400]{2,3,1,0:T(8,128)S(1)}, f32[1,1,256,400]{2,3,1,0:T(8,128)}, u32[]{:S(2)}) copy-start(f32[1,1,256,400]{2,3,1,0:T(8,128)} %param.14) | copy-start | bytes 1228804
  1.6 4.3 %copy-start.2 = (f32[1,1,256,400]{2,3,1,0:T(8,128)S(1)}, f32[1,1,256,400]{2,3,1,0:T(8,128)}, u32[]{:S(2)}) copy-start(f32[1,1,256,400]{2,3,1,0:T(8,128)} %param.12) | copy-start | bytes 1228804
  1.6 4.3 %copy-start.3 = (s32[1,1,2,8,128]{4,3,2,1,0:T(8,128)S(1)}, s32[1,1,2,8,128]{4,3,2,1,0:T(8,128)}, u32[]{:S(2)}) copy-start(s32[1,1,2,8,128]{4,3,2,1,0:T(8,128)} %param.17) | copy-start | bytes 24580
  1.6 4.3 %copy-start.4 = (s32[1,1,2,8,128]{4,3,2,1,0:T(8,128)S(1)}, s32[1,1,2,8,128]{4,3,2,1,0:T(8,128)}, u32[]{:S(2)}) copy-start(s32[1,1,2,8,128]{4,3,2,1,0:T(8,128)} %param.18) | copy-start | bytes 24580
  1.6 4.3 %copy-start.5 = (s32[1,1,2,8,128]{4,3,2,1,0:T(8,128)S(1)}, s32[1,1,2,8,128]{4,3,2,1,0:T(8,128)}, u32[]{:S(2)}) copy-start(s32[1,1,2,8,128]{4,3,2,1,0:T(8,128)} %param.19) | copy-start | bytes 24580
  1.6 4.3 %copy-start.6 = (f32[1,1,256]{2,1,0:T(1,128)S(1)}, f32[1,1,256]{2,1,0:T(1,128)}, u32[]{:S(2)}) copy-start(f32[1,1,256]{2,1,0:T(1,128)} %param.15) | copy-start | bytes 3076
  1.7 4.3 %copy-start.7 = (s32[1,1,2,8]{3,2,1,0:T(2,128)S(1)}, s32[1,1,2,8]{3,2,1,0:T(2,128)}, u32[]{:S(2)}) copy-start(s32[1,1,2,8]{3,2,1,0:T(2,128)} %param.20) | copy-start | bytes 196
  1.7 4.3 %copy-start.8 = (s32[1,1,2,8]{3,2,1,0:T(2,128)S(1)}, s32[1,1,2,8]{3,2,1,0:T(2,128)}, u32[]{:S(2)}) copy-start(s32[1,1,2,8]{3,2,1,0:T(2,128)} %param.21) | copy-start | bytes 196
  1.8 20.6 %collective-permute-start.1 = (s16[416,256]{1,0:T(8,128)(2,1)S(1)}, s16[416,256]{1,0:T(8,128)(2,1)S(1)}, u32[]{:S(2)}, u32[]{:S(2)}) collective-permute-start(s16[416,256]{1,0:T(8,128)(2,1)S(1)} %shard_map.155.near), channel_id=1, source_target_pairs={{508,0},{0,4},{4,8},{8,12},{12,16},{16,20},{20,24},{24,28},{28,32}... | collective-permute-start | bytes 638984 | tf_op jit(solution)/shard_map/ppermute | solution.py:316
  6.0 7.4 %copy-start = (f32[16,400]{1,0:T(8,128)S(1)}, f32[16,400]{1,0:T(8,128)}, u32[]{:S(2)}) copy-start(f32[16,400]{1,0:T(8,128)} %relation.5) | copy-start | bytes 76804
  6.0 7.4 %copy-start.9 = (s32[1,1,256]{2,1,0:T(1,128)S(1)}, s32[1,1,256]{2,1,0:T(1,128)}, u32[]{:S(2)}) copy-start(s32[1,1,256]{2,1,0:T(1,128)} %param.22) | copy-start | bytes 3076
  6.0 7.4 %copy-start.10 = (s32[1,1,256]{2,1,0:T(1,128)S(1)}, s32[1,1,256]{2,1,0:T(1,128)}, u32[]{:S(2)}) copy-start(s32[1,1,256]{2,1,0:T(1,128)} %param.23) | copy-start | bytes 3076
  7.0 19.2 %collective-permute-start = (s16[416,256]{1,0:T(8,128)(2,1)S(1)}, s16[416,256]{1,0:T(8,128)(2,1)S(1)}, u32[]{:S(2)}, u32[]{:S(2)}) collective-permute-start(s16[416,256]{1,0:T(8,128)(2,1)S(1)} %get-tuple-element.38), channel_id=1, source_target_pairs={{504,0},{508,4},{0,8},{4,12},{8,16},{12,20},{16,24},{20,28},{24,32... | collective-permute-start | bytes 638984 | tf_op jit(solution)/shard_map/ppermute | solution.py:316
  10.2 21.2 %collective-permute-start.2 = (s16[416,256]{1,0:T(8,128)(2,1)S(1)}, s16[416,256]{1,0:T(8,128)(2,1)S(1)}, u32[]{:S(2)}, u32[]{:S(2)}) collective-permute-start(s16[416,256]{1,0:T(8,128)(2,1)S(1)} %get-tuple-element.49), channel_id=1, source_target_pairs={{508,0},{0,4},{4,8},{8,12},{12,16},{16,20},{20,24},{24,28},{28,32}... | collective-permute-start | bytes 638984 | tf_op jit(solution)/shard_map/ppermute | solution.py:316
  13.4 9.0 %copy-start.11 = (f32[1,1,256]{2,1,0:T(1,128)S(1)}, f32[1,1,256]{2,1,0:T(1,128)}, u32[]{:S(2)}) copy-start(f32[1,1,256]{2,1,0:T(1,128)} %param.13) | copy-start | bytes 3076
  37.5 11.4 %all-to-all-start = ((bf16[4,208,128]{2,1,0:T(8,128)(2,1)}), bf16[4,208,128]{2,1,0:T(8,128)(2,1)S(1)}, u32[]{:S(2)}, u32[]{:S(2)}) async-start(bf16[4,208,128]{2,1,0:T(8,128)(2,1)} %get-tuple-element.70), calls=%async_computation | async-start | bytes 425984 | tf_op jit(solution)/shard_map/all_to_all | solution.py:368
